TPU v7x, 32 devices: a whole 2x2x4 slice. The times are simulated.
32 devices in a mesh: row: 8 (over y, x, core), col: 4 (over z).
Axes of the slice: x: 2, y: 2, z: 4, core: 2. Of those that a mesh axis runs over, the one named last changes fastest.
Arguments:
- x_mat: float32 [512, 512], replicated, may hold values from -8 to 40, as said below
- y_inv: float32 [512, 512], replicated, may hold values from -8 to 40, as said below
- panel_blocks: bfloat16 [512, 4096], replicated, may hold values from -6 to 6
- panel_pos: int32 [512], replicated, may hold values from 0 to 63
- group_blocks: int32 [32, 2], replicated, may hold values from 0 to 63
- cons_blocks: bfloat16 [57344, 4096], P(('row', 'col')), may hold values from -6 to 6
- slot_block: int32 [57344], P(('row', 'col')), may hold values from 0 to 1
- slot_row: int32 [57344], P(('row', 'col')), may hold values from 0 to 32767, as said below
- group_size: int32 [32], P(('row', 'col')), may hold values from 768 to 1792, as said below
- trailing: float32 [32768, 2048], P('row', 'col'), may hold values from -6 to 6
Outputs:
- lower_panel: float32 [32768, 512], P(('row', 'col'))
- updated: float32 [32768, 2048], P('row', 'col')
Inputs may be any that keep to these rules, and one draw needn't show every extreme that they name: `x_mat`: symmetric positive definite. `y_inv`: symmetric positive definite. `slot_row`: over all groups, the live slots hold every row 0 to 32767 exactly once; the live slots of one group hold at most 56 rows of one aligned range of 1024 rows, and that most is reached in every draw; other slots hold arbitrary rows. `group_size`: the live slots of a group are its first slots; some group has exactly 1792 in every draw.
All inputs are finite; a program needn't handle non-finite values.
Results may differ from a plain program's by a relative error of at most 0.004.
Values may be sent and summed in bfloat16 or wider, within the bound.
A program may use at most 192 MiB of HBM per device.

v0:
```python
import functools
import math

import jax
import jax.numpy as jnp
from jax import lax
from jax.experimental import pallas as pl
from jax.experimental.pallas import tpu as pltpu
from jax.sharding import PartitionSpec as P

BF16 = jnp.bfloat16
F32 = jnp.float32


def split(value):
    high = value.astype(BF16)
    low = (value - high.astype(F32)).astype(BF16)
    return high, low


def halves(block_size, rows):
    return lax.broadcasted_iota(jnp.int32, (rows, 2 * block_size), 1) < block_size


def congruence(p, q, pair, left_ref, high_ref, low_ref):
    block_size = pair.shape[0]
    keep = halves(block_size, block_size)
    zero = jnp.zeros_like(pair)
    first = jnp.where(keep, pair, zero)
    second = jnp.where(keep, zero, pair)
    stacked = jnp.concatenate([first, first, second, second], axis=0)
    left = jnp.concatenate([left_ref[p], left_ref[q]], axis=1)
    inner = jnp.dot(left, stacked, preferred_element_type=F32)
    rows = inner.shape[0] // 2
    wide = jnp.concatenate([inner[:rows], inner[rows:]], axis=1)
    wide_high, wide_low = split(wide)
    z_high = jnp.concatenate([high_ref[0, q], high_ref[0, p], high_ref[1, q], high_ref[1, p]], axis=0)
    z_low = jnp.concatenate([low_ref[0, q], low_ref[0, p], low_ref[1, q], low_ref[1, p]], axis=0)
    dot = functools.partial(jnp.dot, preferred_element_type=F32)
    return dot(wide_high, z_high) + (dot(wide_high, z_low) + dot(wide_low, z_high))


def own_kernel(block_count, pos_ref, pair_ref, left_ref, high_ref, low_ref, out_ref, scr):
    step = pl.program_id(0)
    position = pos_ref[step]
    p = position // block_count
    q = position % block_count
    h = congruence(p, q, pair_ref[0], left_ref, high_ref, low_ref)
    order = h.shape[0]
    block_size = order // block_count
    lanes = 2 * block_size
    groups = order // lanes
    for g in range(groups):
        scr[g * order : (g + 1) * order, :] = h[:, g * lanes : (g + 1) * lanes]
    keep = halves(block_size, block_count)
    for g in range(groups):
        for r in range(0, block_size, 2):
            even = scr[pl.ds(g * order + r, block_count, stride=block_size), :]
            odd = scr[pl.ds(g * order + r + 1, block_count, stride=block_size), :]
            one = jnp.where(keep, even, pltpu.roll(odd, block_size, 1))
            two = jnp.where(keep, pltpu.roll(even, block_size, 1), odd)
            both = jnp.concatenate([one, two], axis=0).astype(BF16)
            out_ref[
                2 * g * block_count : 2 * (g + 1) * block_count,
                r * block_size : (r + 2) * block_size,
            ] = both


def group_kernel(block_count, tile, pos_ref, pair_ref, left_ref, high_ref, low_ref, out_ref, scr):
    step = pl.program_id(0)
    block_size = pair_ref.shape[1]
    keep_rows = halves(block_size, block_size)
    for j in range(tile):
        position = pos_ref[step * tile + j]
        p = position // block_count
        q = position % block_count
        h = congruence(p, q, pair_ref[j], left_ref, high_ref, low_ref)
        scr[j * block_size : (j + 1) * block_size, :] = jnp.where(
            keep_rows, h[:block_size], h[block_size:]
        )
    keep = halves(block_size, tile)
    for r in range(0, block_size, 2):
        even = scr[pl.ds(r, tile, stride=block_size), :]
        odd = scr[pl.ds(r + 1, tile, stride=block_size), :]
        columns = slice(r * block_size, (r + 2) * block_size)
        out_ref[0, :, columns] = jnp.where(keep, even, pltpu.roll(odd, block_size, 1)).astype(BF16)
        out_ref[1, :, columns] = jnp.where(keep, pltpu.roll(even, block_size, 1), odd).astype(BF16)


def whole(shape):
    return pl.BlockSpec(shape, lambda *_: (0,) * len(shape))


def own_table(pairs, positions, left, high, low, block_count):
    count, block_size, lanes = pairs.shape
    order = block_count * block_size
    rows = block_count * block_count
    return pl.pallas_call(
        functools.partial(own_kernel, block_count),
        grid_spec=pltpu.PrefetchScalarGridSpec(
            num_scalar_prefetch=1,
            grid=(count,),
            in_specs=[
                pl.BlockSpec((1, block_size, lanes), lambda i, _: (i, 0, 0)),
                whole(left.shape),
                whole(high.shape),
                whole(low.shape),
            ],
            out_specs=pl.BlockSpec((rows, block_size * block_size), lambda i, _: (i, 0)),
            scratch_shapes=[pltpu.VMEM((order * order // lanes, lanes), F32)],
        ),
        out_shape=jax.ShapeDtypeStruct((count * rows, block_size * block_size), BF16),
        name="own_table",
    )(positions, pairs, left, high, low)


def group_table(pairs, positions, left, high, low, block_count):
    count, block_size, lanes = pairs.shape
    tile = 16
    return pl.pallas_call(
        functools.partial(group_kernel, block_count, tile),
        grid_spec=pltpu.PrefetchScalarGridSpec(
            num_scalar_prefetch=1,
            grid=(count // tile,),
            in_specs=[
                pl.BlockSpec((tile, block_size, lanes), lambda i, _: (i, 0, 0)),
                whole(left.shape),
                whole(high.shape),
                whole(low.shape),
            ],
            out_specs=pl.BlockSpec((2, tile, block_size * block_size), lambda i, _: (0, i, 0)),
            scratch_shapes=[pltpu.VMEM((tile * block_size, lanes), F32)],
        ),
        out_shape=jax.ShapeDtypeStruct((2, count, block_size * block_size), BF16),
        cost_estimate=pl.CostEstimate(
            flops=40 * 10**9, bytes_accessed=20 * 10**6, transcendentals=0
        ),
        name="group_table",
    )(positions, pairs, left, high, low)


def hdot(a, b, contract):
    return lax.dot_general(
        a, b, ((contract[:1], contract[1:]), ((), ())),
        precision=lax.Precision.HIGHEST, preferred_element_type=F32,
    )


def factor_kernel(block, s_ref, out_ref, a, work):
    order = s_ref.shape[0]
    count = order // block
    groups = block // 8
    a[...] = s_ref[...]
    row_id = lax.broadcasted_iota(jnp.int32, (8, 1), 0)
    eye = (
        lax.broadcasted_iota(jnp.int32, (block, block), 0)
        == lax.broadcasted_iota(jnp.int32, (block, block), 1)
    ).astype(F32)

    def diagonal(b, carry):
        start = pl.multiple_of(b * block, block)
        work[:, :block] = a[pl.ds(start, block), pl.ds(start, block)]
        work[:, block:] = eye
        rows = [work[8 * g : 8 * g + 8, :] for g in range(groups)]
        for k in range(block):
            g, s = divmod(k, 8)
            pivot_row = rows[g][s : s + 1, :]
            d = pivot_row[:, k : k + 1]
            inv = lax.rsqrt(d)
            inv = inv * (1.5 - 0.5 * d * inv * inv)
            scaled = pivot_row * inv
            for i in range(g, groups):
                mult = rows[i][:, k : k + 1] * inv
                if i == g:
                    mult = jnp.where(row_id > s, mult, 0.0)
                    rows[i] = jnp.where(row_id == s, scaled, rows[i] - mult * scaled)
                else:
                    rows[i] = rows[i] - mult * scaled
        inverse = jnp.concatenate([row[:, block:] for row in rows], axis=0)
        out_ref[pl.ds(start, block), pl.ds(start, block)] = inverse
        panel = hdot(a[:, pl.ds(start, block)], inverse, (1, 1))
        below = lax.broadcasted_iota(jnp.int32, (order, 1), 0) >= start + block
        panel = jnp.where(below, panel, 0.0)
        a[:, pl.ds(start, block)] = panel
        return carry, panel

    def body(b, carry):
        _, panel = diagonal(b, carry)
        start = pl.multiple_of(b * block, block)

        for i in range(1, count):
            @pl.when(b < i)
            def _():
                piece = a[i * block : (i + 1) * block, pl.ds(start, block)]
                cols = slice(i * block, (i + 1) * block)
                a[:, cols] = a[:, cols] - hdot(panel, piece, (1, 1))

        return carry

    lax.fori_loop(0, count, body, 0)
    for i in range(count):
        for b in range(i + 1, count):
            out_ref[i * block : (i + 1) * block, b * block : (b + 1) * block] = jnp.zeros(
                (block, block), F32
            )
    for i in range(1, count):
        low_row = a[i * block : (i + 1) * block, : i * block]
        total = hdot(low_row, out_ref[: i * block, : i * block], (1, 0))
        own = out_ref[i * block : (i + 1) * block, i * block : (i + 1) * block]
        out_ref[i * block : (i + 1) * block, : i * block] = -hdot(own, total, (1, 0))


def inverse_factor(matrix):
    order = matrix.shape[0]
    block = 128
    return pl.pallas_call(
        functools.partial(factor_kernel, block),
        in_specs=[pl.BlockSpec(memory_space=pltpu.VMEM)],
        out_specs=pl.BlockSpec(memory_space=pltpu.VMEM),
        out_shape=jax.ShapeDtypeStruct((order, order), F32),
        scratch_shapes=[pltpu.VMEM((order, order), F32), pltpu.VMEM((block, 2 * block), F32)],
        cost_estimate=pl.CostEstimate(
            flops=60 * 10**9, bytes_accessed=2 * 10**6, transcendentals=order
        ),
        name="inverse_factor",
    )(matrix)


def blocks_of_columns(matrix, block_count):
    rows = matrix.shape[0]
    return matrix.reshape(rows, block_count, -1).transpose(1, 0, 2)


def body(
    x_mat,
    y_inv,
    panel_blocks,
    panel_pos,
    group_blocks,
    cons_blocks,
    slot_block,
    slot_row,
    group_size,
    trailing,
):
    rows_size = lax.axis_size("row")
    cols_size = lax.axis_size("col")
    devices = rows_size * cols_size
    col_index = lax.axis_index("col")
    device_id = lax.axis_index("row") * cols_size + col_index
    panel_cols = panel_blocks.shape[0]
    per_device = panel_cols // devices
    order = x_mat.shape[0]
    block_size = math.isqrt(panel_blocks.shape[1])
    block_count = order // block_size
    square = panel_blocks.reshape(panel_cols, block_size, block_size)
    pairs = jnp.concatenate([square, square.transpose(0, 2, 1)], axis=2)
    both = jnp.stack([y_inv, x_mat])
    rounded = lax.reduce_precision(both, exponent_bits=8, mantissa_bits=7)
    both_high = rounded.astype(BF16)
    both_low = lax.reduce_precision(both - rounded, exponent_bits=8, mantissa_bits=7).astype(BF16)
    high = both_high.reshape(2, block_count, block_size, order)
    low = both_low.reshape(2, block_count, block_size, order)
    tall_high = jnp.concatenate([both_high[1], both_high[0]], axis=0)
    tall_low = jnp.concatenate([both_low[1], both_low[0]], axis=0)
    left = jnp.concatenate(
        [blocks_of_columns(tall_high, block_count), blocks_of_columns(tall_low, block_count)], axis=2
    )
    own_pairs = lax.dynamic_slice_in_dim(pairs, device_id * per_device, per_device, 0)
    own_pos = lax.dynamic_slice_in_dim(panel_pos, device_id * per_device, per_device, 0)
    own_rows = own_table(own_pairs, own_pos, left, high, low, block_count)
    products = lax.dot_general(
        own_rows, panel_blocks, (((1,), (1,)), ((), ())), preferred_element_type=F32
    )
    place = panel_pos % block_count * block_count + panel_pos // block_count
    position_count = block_count * block_count
    hit = jnp.arange(position_count, dtype=jnp.int32)[:, None] == place[None, :]
    row_part = jnp.sum(
        jnp.where(hit[None], products.reshape(per_device, position_count, panel_cols), 0.0), axis=1
    )
    panel_schur = lax.all_gather(row_part, ("row", "col"), axis=0, tiled=True)

    own_group = lax.dynamic_index_in_dim(group_blocks, device_id, 0, keepdims=False)
    slots = own_group.shape[0]
    lefts, highs, lows = [], [], []
    for slot_index in range(slots):
        a_block = own_group[slot_index] // block_count
        b_start = own_group[slot_index] % block_count * block_size
        lefts.append(
            lax.dynamic_slice_in_dim(
                left.reshape(block_count, 2, order, 2 * block_size), a_block * block_size, block_size, 2
            )
        )
        highs.append(lax.dynamic_slice_in_dim(high, b_start, block_size, 3))
        lows.append(lax.dynamic_slice_in_dim(low, b_start, block_size, 3))
    group_left = jnp.concatenate(lefts, axis=2).reshape(
        block_count, 2 * slots * block_size, 2 * block_size
    )
    group_rows = group_table(
        pairs, panel_pos, group_left, jnp.concatenate(highs, axis=3), jnp.concatenate(lows, axis=3),
        block_count,
    )
    slot_count = cons_blocks.shape[0]
    running = None
    for slot_index in range(slots):
        product_part = lax.dot_general(
            cons_blocks, group_rows[slot_index], (((1,), (1,)), ((), ())), preferred_element_type=F32
        )
        if running is None:
            running = jnp.where((slot_block == slot_index)[:, None], product_part, 0.0)
        else:
            running = jnp.where((slot_block == slot_index)[:, None], product_part, running)
    schur_rows = running

    sub_rows = trailing.shape[0] // cols_size
    base_share = sub_rows // devices
    spread = sub_rows - devices // 4 * base_share
    capacity = base_share + (spread + devices - 1) // devices
    live_slots = jnp.arange(slot_count, dtype=jnp.int32) < group_size[0]
    target = slot_row // sub_rows
    dest_hits = (
        (target[:, None] == jnp.arange(devices, dtype=jnp.int32)[None, :]) & live_slots[:, None]
    ).astype(jnp.int32)
    before = jnp.cumsum(dest_hits, axis=0) - dest_hits
    dest_rank = jnp.sum(before * dest_hits, axis=1)
    slot_place = jnp.where(live_slots, target * capacity + dest_rank, devices * capacity)
    place_ids = jnp.arange(devices * capacity, dtype=jnp.int32)
    send_hits = (place_ids[:, None] == slot_place[None, :]).astype(BF16)
    send_rows = jnp.dot(
        send_hits, schur_rows.astype(BF16), preferred_element_type=F32
    ).astype(BF16)
    send_local = (
        jnp.full((devices * capacity,), sub_rows, jnp.int32)
        .at[slot_place]
        .set(slot_row % sub_rows, mode="drop")
    )
    exchange = functools.partial(
        lax.all_to_all, axis_name=("row", "col"), split_axis=0, concat_axis=0, tiled=True
    )
    recv_local = exchange(send_local.reshape(devices, capacity))
    recv_rows = exchange(send_rows.reshape(devices, capacity, panel_cols))
    symmetric = 0.5 * (panel_schur + panel_schur.T)
    diag_shift = 0.01 * jnp.mean(jnp.diagonal(symmetric))
    inverse = inverse_factor(symmetric + diag_shift * jnp.eye(panel_cols, dtype=F32))
    local_ids = jnp.arange(sub_rows, dtype=jnp.int32)
    recv_hits = (local_ids[:, None] == recv_local.reshape(1, -1)).astype(BF16)
    row_slab = jnp.dot(
        recv_hits, recv_rows.reshape(-1, panel_cols), preferred_element_type=F32
    )
    lower_slab = hdot(row_slab, inverse, (1, 1))
    all_rows = lax.all_gather(lower_slab.astype(BF16), "col", axis=0, tiled=True)
    block_rows = trailing.shape[1] // rows_size
    own_rows = lax.dynamic_slice_in_dim(all_rows, col_index * block_rows, block_rows, 0)
    picked = lax.all_gather(own_rows, "row", axis=0, tiled=True)
    update = lax.dot_general(
        all_rows, picked, (((1,), (1,)), ((), ())), preferred_element_type=F32
    )
    return (lower_slab, trailing - update)


def solution(mesh):
    return jax.shard_map(
        body,
        mesh=mesh,
        in_specs=(
            P(),
            P(),
            P(),
            P(),
            P(),
            P(("row", "col"), None),
            P(("row", "col")),
            P(("row", "col")),
            P(("row", "col")),
            P("row", "col"),
        ),
        out_specs=(P(("row", "col"), None), P("row", "col")),
        check_vma=False,
    )
```

profile of v0, /device:TPU:0, one launch (start us, length us, event | category | flops | bytes accessed | tf_op | source)
XLA Modules:
  0.0 513.4 jit_solution(11813711501293940192)
XLA Ops:
  7.2 6.5 %copy.28 = bf16[512,4096]{0,1:T(8,128)(2,1)} copy(bf16[512,4096]{1,0:T(8,128)(2,1)} %param.12) | data formatting | bytes 8388608 | tf_op args[2]
  13.7 15.6 %copy.29 = bf16[512,64,64]{1,2,0:T(8,128)(2,1)} copy(bf16[512,64,64]{0,2,1:T(8,128)(2,1)} %bitcast.74) | data formatting | bytes 8388608 | tf_op jit(solution)/shard_map/reshape | solution.py:256
  29.3 13.1 %copy.30 = bf16[512,64,64]{2,1,0:T(8,128)(2,1)} copy(bf16[512,64,64]{0,2,1:T(8,128)(2,1)} %bitcast.75) | data formatting | bytes 8388608 | tf_op jit(solution)/shard_map/reshape | solution.py:256
  49.2 2.5 copy.34
  51.7 2.3 copy.35
  54.0 2.4 copy.36
  60.3 2.5 pad_maximum_fusion.2.left_ref
  64.6 29.1 %own_table.1 = bf16[1024,4096]{1,0:T(8,128)(2,1)} custom-call(s32[16]{0:T(128)} %dynamic_slice.38.pos_ref, bf16[16,64,128]{2,1,0:T(8,128)(2,1)} %fusion.15.pair_ref, bf16[8,1024,128]{2,1,0:T(8,128)(2,1)} %pad_maximum_fusion.2.left_ref, bf16[2,8,64,512]{3,2,1,0:T(8,128)(2,1)} %get-tuple-element.5.high_ref, bf16[2,8,64,512]{3,2,1,0:T(8,128)(2,1)} %get-tuple-element.4.low_ref), custom_call_target="tpu_custom_call" | custom-call | tf_op jit(solution)/shard_map/own_table/pallas_call | solution.py:98
  93.7 9.7 %select_reduce_fusion = f32[16,512]{1,0:T(8,128)} fusion(pred[64,512]{1,0:T(8,128)(4,1)S(1)} %iota_compare_fusion.9, bf16[1024,4096]{1,0:T(8,128)(2,1)} %own_table.1, bf16[512,4096]{1,0:T(8,128)(2,1)} %param.12), kind=kOutput, calls=%fused_computation.31 | convolution fusion | flops 4296007680 | bytes 12648448 | tf_op jit(solution)/shard_map/dot_general | solution.py:272
  104.2 9.1 %reduce-window.6 = s32[32,14,128]{2,1,0:T(8,128)S(1)} reduce-window(s32[32,14,128]{2,1,0:T(8,128)S(1)} %fusion.17, s32[]{:T(128)} %constant.112.clone.1), window={size=1x1x128 pad=0_0x0_0x127_0}, to_apply=%region_0.1 | reduce-window | flops 7282688 | bytes 458756 | tf_op jit(solution)/shard_map/reduce-window
  114.0 7.1 %scatter_custom_fusion = s32[1792]{0:T(1024)S(1)} fusion(s32[1792]{0:T(1024)S(1)} %get-tuple-element.2, s32[1792]{0:T(1024)S(1)} %get-tuple-element.18, s32[]{:T(128)} %constant.110.clone.1), kind=kCustom, calls=%fused_computation.68 | custom fusion | bytes 7172 | tf_op jit(solution)/shard_map/scatter | solution.py:335
  121.8 7.8 %all-to-all-start = ((s32[32,1,56]{2,1,0:T(1,128)}), s32[32,1,56]{2,1,0:T(1,128)S(1)}, u32[]{:S(2)}, u32[]{:S(2)}) async-start(s32[32,1,56]{2,1,0:T(1,128)} %all_to_all.9), calls=%async_computation | async-start | bytes 32768 | tf_op jit(solution)/shard_map/all_to_all | solution.py:340
  135.2 11.0 %pad_maximum_fusion.pair_ref = bf16[512,64,128]{2,1,0:T(8,128)(2,1)} fusion(bf16[512,64,64]{2,1,0:T(8,128)(2,1)} %bitcast.73, bf16[512,64,64]{2,1,0:T(8,128)(2,1)} %copy.30), kind=kLoop, calls=%fused_computation.5 | loop fusion | flops 16777216 | bytes 16777216 | tf_op jit(solution)/shard_map/concatenate | solution.py:257
  150.3 139.4 %group_table.1 = bf16[2,512,4096]{2,1,0:T(8,128)(2,1)} custom-call(s32[512]{0:T(512)} %pos_ref.1, bf16[512,64,128]{2,1,0:T(8,128)(2,1)} %pad_maximum_fusion.pair_ref, bf16[8,256,128]{2,1,0:T(8,128)(2,1)} %bitcast.87, bf16[2,8,64,128]{3,2,1,0:T(8,128)(2,1)} %pad_maximum_fusion.5.high_ref, bf16[2,8,64,128]{3,2,1,0:T(8,128)(2,1)} %pad_maximum_fusion.6.low_ref), custom_call_target="tpu_custom_call" | custom-call | flops 40000000000 | bytes 20000000 | tf_op jit(solution)/shard_map/group_table/pallas_call | solution.py:120
  289.7 13.4 %fusion.3 = bf16[512,1792]{1,0:T(8,128)(2,1)S(1)} fusion(bf16[1792,4096]{1,0:T(8,128)(2,1)} %param.15, bf16[2,512,4096]{2,1,0:T(8,128)(2,1)} %group_table.1), kind=kOutput, calls=%fused_computation.12 | convolution fusion | flops 7516192768 | bytes 20709376 | tf_op jit(solution)/shard_map/dot_general | solution.py:306
  303.1 18.8 %fusion.6 = bf16[1792,512]{1,0:T(8,128)(2,1)} fusion(bf16[512,1792]{1,0:T(8,128)(2,1)S(1)} %fusion.3, bf16[1792,4096]{1,0:T(8,128)(2,1)} %param.15, bf16[2,512,4096]{2,1,0:T(8,128)(2,1)} %group_table.1, s32[1792]{0:T(1024)S(1)} %get-tuple-element.3, pred[1792]{0:T(1024)(128)(4,1)S(1)} %get-tuple-element.21, pred[1792]{0:T(1024)(128)(4,1)S(1)} %get-tuple-element.20), kind=kOutput, calls=%fused_computation.21 | convolution fusion | flops 10810490880 | bytes 22555136 | tf_op jit(solution)/shard_map/dot_general | solution.py:329
  321.9 6.0 %all-to-all-start.1 = ((bf16[32,56,512]{2,1,0:T(8,128)(2,1)}), bf16[32,56,512]{2,1,0:T(8,128)(2,1)}, u32[]{:S(2)}, u32[]{:S(2)}) async-start(bf16[32,56,512]{2,1,0:T(8,128)(2,1)} %bitcast.22), calls=%async_computation.1 | async-start | bytes 3670016 | tf_op jit(solution)/shard_map/all_to_all | solution.py:341
  332.4 4.5 gather_fusion
  339.2 55.1 %inverse_factor.1 = f32[512,512]{1,0:T(8,128)} custom-call(f32[512,512]{1,0:T(8,128)} %select_add_fusion.s_ref), custom_call_target="tpu_custom_call" | custom-call | flops 60000002048 | bytes 2000000 | tf_op jit(solution)/shard_map/inverse_factor/pallas_call | solution.py:216
  394.3 3.6 fusion.1
  398.0 5.1 fusion.34
  403.2 82.1 %all-gather.5.cloned.1.call-done = bf16[4096,512]{1,0:T(8,128)(2,1)} async-done(((bf16[1024,512]{1,0:T(8,128)(2,1)}), bf16[4096,512]{1,0:T(8,128)(2,1)}) %all-gather.5.cloned.1.call-update) | async-done | bytes 4194320 | tf_op jit(solution)/shard_map/all_gather | solution.py:351
  486.1 9.8 %all_gather.11 = bf16[512,512]{1,0:T(8,128)(2,1)S(1)} all-gather(bf16[64,512]{1,0:T(8,128)(2,1)S(1)} %constant_dynamic-slice_fusion), channel_id=1, replica_groups=mesh['row'=8,'col'=4] {'row'}, dimensions={0}, use_global_device_ids=true | all-gather | bytes 589824 | tf_op jit(solution)/shard_map/all_gather | solution.py:354
  495.9 10.4 %convolution_subtract_fusion = f32[4096,512]{1,0:T(8,128)} fusion(f32[4096,512]{1,0:T(8,128)} %param.19, bf16[4096,512]{1,0:T(8,128)(2,1)} %all-gather.5.cloned.1.call-done, bf16[512,512]{1,0:T(8,128)(2,1)S(1)} %all_gather.11), kind=kOutput, calls=%fused_computation.10 | convolution fusion | flops 2149580800 | bytes 21495808 | tf_op jit(solution)/shard_map/dot_general | solution.py:355
  (74 shorter events, 25.6 us)
Async XLA Ops:
  7.2 122.5 %copy-start = (s32[32,2]{0,1:T(2,128)S(1)}, s32[32,2]{0,1:T(2,128)}, u32[]{:S(2)}) copy-start(s32[32,2]{0,1:T(2,128)} %param.14) | copy-start | bytes 772
  7.2 322.1 %all-gather.3.cloned.1.call-start = ((), (), s32[]{:S(2)}) async-start(), calls=%async_computation.2 | async-start | bytes 1081344 | tf_op jit(solution)/shard_map/all_gather | solution.py:281
  29.3 13.1 %copy-start.12 = (s32[512]{0:T(512)S(1)}, s32[512]{0:T(512)}, u32[]{:S(2)}) copy-start(s32[512]{0:T(512)} %pos_ref.1) | copy-start | bytes 6148
  29.3 13.8 %copy-start.5 = (f32[512,512]{1,0:T(8,128)S(1)}, f32[512,512]{1,0:T(8,128)}, u32[]{:S(2)}) copy-start(f32[512,512]{1,0:T(8,128)} %param.11) | copy-start | bytes 3145732
  29.3 14.1 %copy-start.4 = (f32[512,512]{1,0:T(8,128)S(1)}, f32[512,512]{1,0:T(8,128)}, u32[]{:S(2)}) copy-start(f32[512,512]{1,0:T(8,128)} %param.10) | copy-start | bytes 3145732
  56.4 2.0 copy-start.6
  58.4 1.2 copy-start.7
  58.4 1.5 copy-start.8
  93.7 9.8 %copy-start.10 = (s32[1792]{0:T(1024)S(1)}, s32[1792]{0:T(1024)}, u32[]{:S(2)}) copy-start(s32[1792]{0:T(1024)} %param.17) | copy-start | bytes 21508
  121.8 200.1 %all-to-all-start = ((s32[32,1,56]{2,1,0:T(1,128)}), s32[32,1,56]{2,1,0:T(1,128)S(1)}, u32[]{:S(2)}, u32[]{:S(2)}) async-start(s32[32,1,56]{2,1,0:T(1,128)} %all_to_all.9), calls=%async_computation | async-start | bytes 32768 | tf_op jit(solution)/shard_map/all_to_all | solution.py:340
  135.1 11.0 %copy-start.11 = (s32[1792]{0:T(1024)S(1)}, s32[1792]{0:T(1024)}, u32[]{:S(2)}) copy-start(s32[1792]{0:T(1024)} %param.16) | copy-start | bytes 21508
  135.1 13.0 %copy-start.2 = (bf16[2,8,64,512]{3,2,1,0:T(8,128)(2,1)S(1)}, bf16[2,8,64,512]{3,2,1,0:T(8,128)(2,1)}, u32[]{:S(2)}) copy-start(bf16[2,8,64,512]{3,2,1,0:T(8,128)(2,1)} %get-tuple-element.4.low_ref) | copy-start | bytes 3145732
  135.1 13.0 %copy-start.3 = (bf16[2,8,64,512]{3,2,1,0:T(8,128)(2,1)S(1)}, bf16[2,8,64,512]{3,2,1,0:T(8,128)(2,1)}, u32[]{:S(2)}) copy-start(bf16[2,8,64,512]{3,2,1,0:T(8,128)(2,1)} %get-tuple-element.5.high_ref) | copy-start | bytes 3145732
  321.9 72.4 %all-to-all-start.1 = ((bf16[32,56,512]{2,1,0:T(8,128)(2,1)}), bf16[32,56,512]{2,1,0:T(8,128)(2,1)}, u32[]{:S(2)}, u32[]{:S(2)}) async-start(bf16[32,56,512]{2,1,0:T(8,128)(2,1)} %bitcast.22), calls=%async_computation.1 | async-start | bytes 3670016 | tf_op jit(solution)/shard_map/all_to_all | solution.py:341
  327.9 157.3 %all-gather.5.cloned.1.call-start = ((), (), s32[]{:S(2)}) async-start(), calls=%async_computation.3 | async-start | bytes 5242880 | tf_op jit(solution)/shard_map/all_gather | solution.py:351
  394.3 3.7 copy-start.9
  495.9 10.5 %copy-start.1 = (s32[32,2]{0,1:T(2,128)S(1)}, s32[32,2]{0,1:T(2,128)}, u32[]{:S(2)}) copy-start(s32[32,2]{0,1:T(2,128)} %param.14) | copy-start | bytes 772
Sparse Core Ops, SparseCore 0:
  103.6 56.5 all-gather.2
  403.3 81.8 all-gather.4
where the time goes:
time: 521 us; the launch traced here: 513 us
  Pallas kernels  224 us (43%)
  waiting for transfers between devices  82.1 us (16%)
  local copies, waits for them, and re-layouts  66.6 us (13%)
  matrix products  61.1 us (12%)
  other arithmetic  35.5 us (7%)
  between operations  20.7 us (4%)
  starting transfers between devices  14 us (3%)
  blocking collectives  9.8 us (2%)
    pallas_call x1, Pallas kernels, group_table(): pl.pallas_call(functools.partial(group_kernel, block_count, tile), grid_s...  139 us
    all_gather x1, waiting for transfers between devices, body(): lax.all_gather(lower_slab.astype(BF16), 'col', axis=0, tiled=True)  82.1 us
    pallas_call x1, Pallas kernels, inverse_factor(): pl.pallas_call(functools.partial(factor_kernel, block), in_specs=[pl.Bloc...  55.1 us
    pallas_call x1, Pallas kernels, own_table(): pl.pallas_call(functools.partial(own_kernel, block_count), grid_spec=pltp...  29.1 us
    reshape x2, local copies, waits for them, and re-layouts, body(): square = panel_blocks.reshape(panel_cols, block_size, block_size)  28.7 us
    dot_general x1, matrix products, body(): jnp.dot(send_hits, schur_rows.astype(BF16), preferred_element_type=F32)  18.8 us
    dot_general x1, matrix products, body(): lax.dot_general(cons_blocks, group_rows[slot_index], (((1,), (1,)), ((),...  13.4 us
    concatenate x2, other arithmetic, body(): pairs = jnp.concatenate([square, square.transpose(0, 2, 1)], axis=2)  13 us
  transfers between devices with their start and end apart: 4, of which 1 were waited for; matrix products, arithmetic and copies ran while one was open for 15% of the time, Pallas kernels for 38%

commit v1 on v0

v1 whole, which is shorter than its diff:
```python
import functools
import math

import jax
import jax.numpy as jnp
from jax import lax
from jax.experimental import pallas as pl
from jax.experimental.pallas import tpu as pltpu
from jax.sharding import PartitionSpec as P

BF16 = jnp.bfloat16
F32 = jnp.float32


def split(value):
    high = value.astype(BF16)
    low = (value - high.astype(F32)).astype(BF16)
    return high, low

def lane_half(rows, width):
    return lax.broadcasted_iota(jnp.int32, (rows, width), 1) < width // 2

def unpack_pairs(panel_ref, pairs, count, block_size):
    lanes = 2 * block_size
    keep = lane_half(count, lanes)
    for c in range(block_size // 2):
        both = panel_ref[:, c * lanes : (c + 1) * lanes].astype(F32)
        turned = pltpu.roll(both, block_size, 1)
        pitch = block_size + 1
        pairs[pl.ds(2 * c, count, stride=pitch), :] = jnp.where(keep, both, turned)
        pairs[pl.ds(2 * c + 1, count, stride=pitch), :] = jnp.where(keep, turned, both)

def column_block(ref, block, slot, block_size):
    lanes = 2 * block_size
    start = pl.multiple_of(block // 2 * lanes, lanes)
    wide = ref[:, pl.ds(start, lanes)]
    return jnp.where(block % 2 == slot, wide, pltpu.roll(wide, block_size, 1))

def group_kernel(block_count, tile, pos_ref, own_ref, x_ref, y_ref, panel_ref, out_ref, left, right, pairs, scr, mid):
    step = pl.program_id(0)
    order = x_ref.shape[0]
    block_size = order // block_count
    lanes = 2 * block_size
    half = lane_half(order, lanes)

    @pl.when(step == 0)
    def _():
        for s in range(2):
            position = own_ref[s]
            a = pl.multiple_of(position // block_count * block_size, block_size)
            xa = x_ref[pl.ds(a, block_size), :]
            ya = y_ref[pl.ds(a, block_size), :]
            for p in range(block_count):
                cols = slice(p * block_size, (p + 1) * block_size)
                high, low = split(jnp.concatenate([xa[:, cols], ya[:, cols]], axis=1))
                left[p, s * block_size : (s + 1) * block_size, :] = high
                left[p, (2 + s) * block_size : (3 + s) * block_size, :] = low
        for m, ref in enumerate((y_ref, x_ref)):
            first = column_block(ref, own_ref[0] % block_count, 0, block_size)
            second = column_block(ref, own_ref[1] % block_count, 1, block_size)
            high, low = split(jnp.where(half, first, second))
            for q in range(block_count):
                rows = slice(q * block_size, (q + 1) * block_size)
                cols = slice(m * lanes, (m + 1) * lanes)
                right[q, :block_size, cols] = high[rows]
                right[q, block_size:, cols] = low[rows]

    unpack_pairs(panel_ref, pairs, tile, block_size)
    keep = lane_half(block_size, lanes)
    dot = functools.partial(jnp.dot, preferred_element_type=F32)

    def spread(j, e, t):
        position = pos_ref[step * tile + j]
        p = position // block_count
        q = position % block_count
        top = dot(e, right[q])
        low_part = dot(t, right[p])
        for m, part in enumerate((top[:, :lanes], top[:, lanes:], low_part[:, :lanes], low_part[:, lanes:])):
            high, low = split(part)
            rows = slice(m * block_size, (m + 1) * block_size)
            mid[j, rows, :lanes] = high
            mid[j, rows, lanes:] = low

    def two(i, carry):
        pitch = block_size + 1
        block = jnp.concatenate(
            [pairs[pl.ds(2 * i * pitch, block_size), :], pairs[pl.ds((2 * i + 1) * pitch, block_size), :]],
            axis=0,
        )
        turned = block.T[:block_size]
        swapped = pltpu.roll(turned, block_size, 1)
        e = block.astype(BF16)
        spread(2 * i, e[:block_size], jnp.where(keep, turned, swapped).astype(BF16))
        spread(2 * i + 1, e[block_size:], jnp.where(keep, swapped, turned).astype(BF16))
        return carry

    lax.fori_loop(0, tile // 2, two, 0, unroll=tile // 2)

    def collect(j, carry):
        position = pos_ref[step * tile + j]
        a = jnp.concatenate([left[position // block_count], left[position % block_count]], axis=1)
        h = dot(a, mid[j])
        b = block_size
        quad = lambda r, c: jnp.where(
            keep, h[r : r + b, c : c + lanes], h[r + b : r + 2 * b, c : c + lanes]
        )
        scr[pl.ds(j * (b + 1), b), :] = quad(0, 0) + (quad(0, lanes) + quad(2 * b, 0))
        return carry

    lax.fori_loop(0, tile, collect, 0, unroll=tile)
    keep_t = lane_half(tile, lanes)
    for r in range(0, block_size, 2):
        even = scr[pl.ds(r, tile, stride=block_size + 1), :]
        odd = scr[pl.ds(r + 1, tile, stride=block_size + 1), :]
        columns = slice(r * block_size, (r + 2) * block_size)
        out_ref[0, :, columns] = jnp.where(keep_t, even, pltpu.roll(odd, block_size, 1)).astype(BF16)
        out_ref[1, :, columns] = jnp.where(keep_t, pltpu.roll(even, block_size, 1), odd).astype(BF16)

def whole(shape):
    return pl.BlockSpec(shape, lambda *_: (0,) * len(shape))


def cost(us, count):
    return pl.CostEstimate(flops=us * 10**9, bytes_accessed=count, transcendentals=0)


def group_table(x, y, panel, positions, own, block_count):
    count, width = panel.shape
    b = x.shape[0] // block_count
    tile = math.gcd(count, 32)
    return pl.pallas_call(
        functools.partial(group_kernel, block_count, tile),
        grid_spec=pltpu.PrefetchScalarGridSpec(
            num_scalar_prefetch=2,
            grid=(count // tile,),
            in_specs=[
                whole(x.shape),
                whole(y.shape),
                pl.BlockSpec((tile, width), lambda i, *_: (i, 0)),
            ],
            out_specs=pl.BlockSpec((2, tile, width), lambda i, *_: (0, i, 0)),
            scratch_shapes=[
                pltpu.VMEM((block_count, 4 * b, 2 * b), BF16),
                pltpu.VMEM((block_count, 2 * b, 4 * b), BF16),
                pltpu.VMEM((tile * (b + 1) + 7, 2 * b), F32),
                pltpu.VMEM((tile * (b + 1) + 7, 2 * b), F32),
                pltpu.VMEM((tile, 4 * b, 4 * b), BF16),
            ],
        ),
        out_shape=jax.ShapeDtypeStruct((2, count, width), BF16),
        cost_estimate=cost(25, 10**7),
        name="group_table",
    )(positions, own, x, y, panel)


def own_kernel(block_count, pos_ref, x_ref, y_ref, panel_ref, out_ref, left, right, pairs, mid, scr):
    step = pl.program_id(0)
    count = panel_ref.shape[0]
    order = x_ref.shape[0]
    b = order // block_count
    lanes = 2 * b
    pitch = b + 1

    @pl.when(step == 0)
    def _():
        for p in range(block_count):
            cols = slice(p * b, (p + 1) * b)
            high, low = split(jnp.concatenate([x_ref[:, cols], y_ref[:, cols]], axis=1))
            left[p, :, :lanes] = high
            left[p, :, lanes:] = low
        for m, ref in enumerate((y_ref, x_ref)):
            for q in range(block_count):
                high, low = split(ref[q * b : (q + 1) * b, :])
                cols = slice(m * order, (m + 1) * order)
                right[q, :b, cols] = high
                right[q, b:, cols] = low
        unpack_pairs(panel_ref, pairs, count, b)

    dot = functools.partial(jnp.dot, preferred_element_type=F32)
    position = pos_ref[step]
    p = position // block_count
    q = position % block_count
    block = pairs[pl.ds(step * pitch, b), :]
    turned = jnp.concatenate([block, block], axis=0).T[:b]
    top = dot(block.astype(BF16), right[q])
    low_part = dot(turned.astype(BF16), right[p])
    for m, part in enumerate((top[:, :order], top[:, order:], low_part[:, :order], low_part[:, order:])):
        high, low = split(part)
        mid[m * b : (m + 1) * b, :] = high
        mid[(8 + m) * b : (9 + m) * b, :] = low
    mid[4 * b : 8 * b, :] = mid[: 4 * b, :]
    lp, lq = left[p], left[q]
    a = jnp.concatenate([lp[:, :lanes], lq[:, :lanes]], axis=1)
    a_low = jnp.concatenate([lp[:, lanes:], lq[:, lanes:]], axis=1)
    a = jnp.concatenate([a, a_low, a], axis=1)
    groups = order // lanes
    for g in range(groups):
        h = dot(a, mid[:, g * lanes : (g + 1) * lanes])
        for i in range(block_count):
            start = (g * block_count + i) * pitch
            scr[start : start + b, :] = h[i * b : (i + 1) * b]
    keep = lane_half(block_count, lanes)
    for g in range(groups):
        base = g * block_count * pitch
        for r in range(0, b, 2):
            even = scr[pl.ds(base + r, block_count, stride=pitch), :]
            odd = scr[pl.ds(base + r + 1, block_count, stride=pitch), :]
            one = jnp.where(keep, even, pltpu.roll(odd, b, 1))
            two = jnp.where(keep, pltpu.roll(even, b, 1), odd)
            out_ref[
                2 * g * block_count : 2 * (g + 1) * block_count, r * b : (r + 2) * b
            ] = jnp.concatenate([one, two], axis=0).astype(BF16)


def own_table(x, y, panel, positions, block_count):
    count, width = panel.shape
    order = x.shape[0]
    b = order // block_count
    rows = block_count * block_count
    return pl.pallas_call(
        functools.partial(own_kernel, block_count),
        grid_spec=pltpu.PrefetchScalarGridSpec(
            num_scalar_prefetch=1,
            grid=(count,),
            in_specs=[whole(x.shape), whole(y.shape), whole(panel.shape)],
            out_specs=pl.BlockSpec((rows, width), lambda i, *_: (i, 0)),
            scratch_shapes=[
                pltpu.VMEM((block_count, order, 4 * b), BF16),
                pltpu.VMEM((block_count, 2 * b, 2 * order), BF16),
                pltpu.VMEM((max(count, 8) * (b + 1) + 7, 2 * b), F32),
                pltpu.VMEM((12 * b, order), BF16),
                pltpu.VMEM((order // 2 // b * block_count * (b + 1) + 7, 2 * b), F32),
            ],
        ),
        out_shape=jax.ShapeDtypeStruct((count * rows, width), BF16),
        cost_estimate=cost(15, 10**7),
        name="own_table",
    )(positions, x, y, panel)


def row_kernel(cons_ref, table_ref, block_ref, place_ref, out_ref, total):
    step = pl.program_id(0)
    nt = (((1,), (1,)), ((), ()))
    cons = cons_ref[...]
    rows = lax.dot_general(cons, table_ref[0], nt, preferred_element_type=F32)
    block = block_ref[...]
    for s in range(1, table_ref.shape[0]):
        other = lax.dot_general(cons, table_ref[s], nt, preferred_element_type=F32)
        rows = jnp.where(block == s, other, rows)
    rows = rows.astype(BF16)
    places, tile = total.shape[0], cons.shape[0]
    hits = lax.broadcasted_iota(jnp.int32, (places, tile), 0) == place_ref[...]
    part = jnp.dot(jnp.where(hits, 1.0, 0.0).astype(BF16), rows, preferred_element_type=F32)

    @pl.when(step == 0)
    def _():
        total[...] = part

    @pl.when(step > 0)
    def _():
        total[...] += part

    @pl.when(step == pl.num_programs(0) - 1)
    def _():
        out_ref[...] = total[...].astype(BF16)


def send_rows(cons, table, block, place, places):
    slots, width = cons.shape
    cols = table.shape[1]
    tile = math.gcd(slots, 256)
    return pl.pallas_call(
        row_kernel,
        grid=(slots // tile,),
        in_specs=[
            pl.BlockSpec((tile, width), lambda i: (i, 0)),
            pl.BlockSpec(table.shape, lambda i: (0, 0, 0), pipeline_mode=pl.Buffered(1)),
            pl.BlockSpec((tile, 1), lambda i: (i, 0)),
            pl.BlockSpec((1, tile), lambda i: (0, i)),
        ],
        out_specs=whole((places, cols)),
        out_shape=jax.ShapeDtypeStruct((places, cols), BF16),
        scratch_shapes=[pltpu.VMEM((places, cols), F32)],
        cost_estimate=cost(20, 2 * 10**7),
        name="send_rows",
    )(cons, table, block.reshape(-1, 1), place.reshape(1, -1))


def update_kernel(parts, *refs):
    row_refs, (weight_ref, trailing_ref, out_ref) = refs[:parts], refs[parts:]
    rows = jnp.concatenate([ref[...] for ref in row_refs] * 2, axis=1)
    out_ref[...] = trailing_ref[...] - jnp.dot(rows, weight_ref[...], preferred_element_type=F32)


def update(row_parts, weight, trailing):
    rows, cols = trailing.shape
    tile = math.gcd(rows, 512)
    return pl.pallas_call(
        functools.partial(update_kernel, len(row_parts)),
        grid=(rows // tile,),
        in_specs=[pl.BlockSpec((tile, part.shape[1]), lambda i: (i, 0)) for part in row_parts]
        + [whole(weight.shape), pl.BlockSpec((tile, cols), lambda i: (i, 0))],
        out_specs=pl.BlockSpec((tile, cols), lambda i: (i, 0)),
        out_shape=jax.ShapeDtypeStruct((rows, cols), F32),
        cost_estimate=cost(8, 2 * 10**7),
        name="update",
    )(*row_parts, weight, trailing)


def hdot(a, b, contract):
    return lax.dot_general(
        a, b, ((contract[:1], contract[1:]), ((), ())),
        precision=lax.Precision.HIGHEST, preferred_element_type=F32,
    )


def factor_kernel(block, s_ref, out_ref, a, work):
    order = s_ref.shape[0]
    count = order // block
    groups = block // 8
    a[...] = s_ref[...]
    row_id = lax.broadcasted_iota(jnp.int32, (8, 1), 0)
    eye = (
        lax.broadcasted_iota(jnp.int32, (block, block), 0)
        == lax.broadcasted_iota(jnp.int32, (block, block), 1)
    ).astype(F32)

    def diagonal(b, carry):
        start = pl.multiple_of(b * block, block)
        work[:, :block] = a[pl.ds(start, block), pl.ds(start, block)]
        work[:, block:] = eye
        rows = [work[8 * g : 8 * g + 8, :] for g in range(groups)]
        for k in range(block):
            g, s = divmod(k, 8)
            pivot_row = rows[g][s : s + 1, :]
            d = pivot_row[:, k : k + 1]
            inv = lax.rsqrt(d)
            inv = inv * (1.5 - 0.5 * d * inv * inv)
            scaled = pivot_row * inv
            for i in range(g, groups):
                mult = rows[i][:, k : k + 1] * inv
                if i == g:
                    mult = jnp.where(row_id > s, mult, 0.0)
                    rows[i] = jnp.where(row_id == s, scaled, rows[i] - mult * scaled)
                else:
                    rows[i] = rows[i] - mult * scaled
        inverse = jnp.concatenate([row[:, block:] for row in rows], axis=0)
        out_ref[pl.ds(start, block), pl.ds(start, block)] = inverse
        panel = hdot(a[:, pl.ds(start, block)], inverse, (1, 1))
        below = lax.broadcasted_iota(jnp.int32, (order, 1), 0) >= start + block
        panel = jnp.where(below, panel, 0.0)
        a[:, pl.ds(start, block)] = panel
        return carry, panel

    def body(b, carry):
        _, panel = diagonal(b, carry)
        start = pl.multiple_of(b * block, block)

        for i in range(1, count):
            @pl.when(b < i)
            def _():
                piece = a[i * block : (i + 1) * block, pl.ds(start, block)]
                cols = slice(i * block, (i + 1) * block)
                a[:, cols] = a[:, cols] - hdot(panel, piece, (1, 1))

        return carry

    lax.fori_loop(0, count, body, 0)
    for i in range(count):
        for b in range(i + 1, count):
            out_ref[i * block : (i + 1) * block, b * block : (b + 1) * block] = jnp.zeros(
                (block, block), F32
            )
    for i in range(1, count):
        low_row = a[i * block : (i + 1) * block, : i * block]
        total = hdot(low_row, out_ref[: i * block, : i * block], (1, 0))
        own = out_ref[i * block : (i + 1) * block, i * block : (i + 1) * block]
        out_ref[i * block : (i + 1) * block, : i * block] = -hdot(own, total, (1, 0))


def inverse_factor(matrix):
    order = matrix.shape[0]
    block = 128
    return pl.pallas_call(
        functools.partial(factor_kernel, block),
        in_specs=[pl.BlockSpec(memory_space=pltpu.VMEM)],
        out_specs=pl.BlockSpec(memory_space=pltpu.VMEM),
        out_shape=jax.ShapeDtypeStruct((order, order), F32),
        scratch_shapes=[pltpu.VMEM((order, order), F32), pltpu.VMEM((block, 2 * block), F32)],
        cost_estimate=pl.CostEstimate(
            flops=60 * 10**9, bytes_accessed=2 * 10**6, transcendentals=order
        ),
        name="inverse_factor",
    )(matrix)


def body(
    x_mat,
    y_inv,
    panel_blocks,
    panel_pos,
    group_blocks,
    cons_blocks,
    slot_block,
    slot_row,
    group_size,
    trailing,
):
    rows_size = lax.axis_size("row")
    cols_size = lax.axis_size("col")
    devices = rows_size * cols_size
    col_index = lax.axis_index("col")
    device_id = lax.axis_index("row") * cols_size + col_index
    panel_cols = panel_blocks.shape[0]
    per_device = panel_cols // devices
    order = x_mat.shape[0]
    block_size = math.isqrt(panel_blocks.shape[1])
    block_count = order // block_size
    slot_count = cons_blocks.shape[0]

    sub_rows = trailing.shape[0] // cols_size
    base_share = sub_rows // devices
    spread = sub_rows - devices // 4 * base_share
    capacity = base_share + (spread + devices - 1) // devices
    places = devices * capacity
    slot_ids = jnp.arange(slot_count, dtype=jnp.int32)
    live_slots = slot_ids < group_size[0]
    target = slot_row // sub_rows
    dest_hits = (
        target[:, None] == jnp.arange(devices, dtype=jnp.int32)[None, :]
    ) & live_slots[:, None]
    earlier = (slot_ids[:, None] > slot_ids[None, :]).astype(BF16)
    before = jnp.dot(earlier, dest_hits.astype(BF16), preferred_element_type=F32)
    dest_rank = jnp.sum(jnp.where(dest_hits, before, 0.0), axis=1).astype(jnp.int32)
    slot_place = jnp.where(live_slots, target * capacity + dest_rank, places)
    place_ids = jnp.arange(places, dtype=jnp.int32)
    tag = slot_row % sub_rows + 1
    digits = jnp.stack([tag // 32, tag % 32], axis=1).astype(BF16)
    sent_digits = jnp.dot(
        (place_ids[:, None] == slot_place[None, :]).astype(BF16), digits, preferred_element_type=F32
    ).astype(jnp.int32)
    send_local = sent_digits[:, 0] * 32 + sent_digits[:, 1] - 1
    exchange = functools.partial(
        lax.all_to_all, axis_name=("row", "col"), split_axis=0, concat_axis=0, tiled=True
    )
    recv_local = exchange(send_local.reshape(devices, capacity))

    own_panel = lax.dynamic_slice_in_dim(panel_blocks, device_id * per_device, per_device, 0)
    own_pos = lax.dynamic_slice_in_dim(panel_pos, device_id * per_device, per_device, 0)
    own_rows = own_table(x_mat, y_inv, own_panel, own_pos, block_count)
    products = lax.dot_general(
        own_rows, panel_blocks, (((1,), (1,)), ((), ())), preferred_element_type=F32
    )
    place = panel_pos % block_count * block_count + panel_pos // block_count
    position_count = block_count * block_count
    hit = jnp.arange(position_count, dtype=jnp.int32)[:, None] == place[None, :]
    row_part = jnp.sum(
        jnp.where(hit[None], products.reshape(per_device, position_count, panel_cols), 0.0), axis=1
    )
    column_part = lax.all_gather(row_part, "col", axis=0, tiled=True)
    panel_schur = lax.all_gather(column_part, "row", axis=0, tiled=True)

    own_group = lax.dynamic_index_in_dim(group_blocks, device_id, 0, keepdims=False)
    halves = 2
    width = panel_cols // halves
    token = row_part
    local_ids = jnp.arange(sub_rows, dtype=jnp.int32)
    slabs, gathered = [], []
    for half in range(halves):
        cols = slice(half * width, (half + 1) * width)
        x_now, token = lax.optimization_barrier((x_mat, token))
        table = group_table(x_now, y_inv, panel_blocks[cols], panel_pos[cols], own_group, block_count)
        sent = send_rows(cons_blocks, table, slot_block, slot_place, places)
        token = sent
        received = exchange(sent.reshape(devices, capacity, width))
        recv_hits = (local_ids[:, None] == recv_local.reshape(1, -1)).astype(BF16)
        slab = jnp.dot(
            recv_hits, received.reshape(-1, width), preferred_element_type=F32
        ).astype(BF16)
        slabs.append(slab)
        gathered.append(lax.all_gather(slab, "col", axis=0, tiled=True))

    block_rows = trailing.shape[1] // rows_size
    slab = jnp.concatenate(slabs, axis=1)
    head = slab[: block_rows * cols_size].reshape(cols_size, block_rows, panel_cols)
    head = lax.all_to_all(head, "col", split_axis=0, concat_axis=0, tiled=True)[0]
    picked = lax.all_to_all(
        jnp.broadcast_to(head[None], (rows_size, block_rows, panel_cols)),
        "row", split_axis=0, concat_axis=0, tiled=True,
    ).reshape(rows_size * block_rows, panel_cols)

    panel_schur, token = lax.optimization_barrier((panel_schur, token))
    symmetric = 0.5 * (panel_schur + panel_schur.T)
    eye = (
        lax.broadcasted_iota(jnp.int32, symmetric.shape, 0)
        == lax.broadcasted_iota(jnp.int32, symmetric.shape, 1)
    )
    diag_shift = 0.01 * jnp.sum(jnp.where(eye, symmetric, 0.0)) / panel_cols
    inverse = inverse_factor(symmetric + jnp.where(eye, diag_shift, 0.0))
    inner = hdot(inverse, inverse, (0, 0))

    def doubled(matrix):
        rounded = lax.reduce_precision(matrix, exponent_bits=8, mantissa_bits=7)
        low = lax.reduce_precision(matrix - rounded, exponent_bits=8, mantissa_bits=7)
        return jnp.concatenate([rounded.astype(BF16), low.astype(BF16)], axis=1)

    lower_slab = lax.dot_general(
        jnp.concatenate([slab, slab], axis=1), doubled(inverse), (((1,), (1,)), ((), ())),
        preferred_element_type=F32,
    )
    weight = lax.dot_general(
        doubled(inner), jnp.concatenate([picked, picked], axis=1), (((1,), (1,)), ((), ())),
        preferred_element_type=F32,
    )
    weight = doubled(weight.T).T
    return (lower_slab, update(gathered, weight, trailing))


def solution(mesh):
    return jax.shard_map(
        body,
        mesh=mesh,
        in_specs=(
            P(),
            P(),
            P(),
            P(),
            P(),
            P(("row", "col"), None),
            P(("row", "col")),
            P(("row", "col")),
            P(("row", "col")),
            P("row", "col"),
        ),
        out_specs=(P(("row", "col"), None), P("row", "col")),
        check_vma=False,
    )
```

time: 521 us -> 332 us (0.64); the launches traced: 513 us -> 331 us
  waiting for transfers between devices: 82.1 us -> 6.91 us
  local copies, waits for them, and re-layouts: 66.6 us -> 14 us
  blocking collectives: 9.8 us -> 62.4 us
  Pallas kernels: 224 us -> 181 us
  matrix products: 61.1 us -> 23.7 us
  other arithmetic: 35.5 us -> 6.71 us
  starting transfers between devices: 14 us -> 21.6 us
  between operations: 20.7 us -> 15.3 us
    pallas_call x1 -> x2, Pallas kernels: 139 us -> 54 us  [group_table(): pl.pallas_call(functools.partial(group_kernel, block_count, tile), grid_s...]
    all_gather x2 -> x3, waiting for transfers between devices: 82.1 us -> 0.01 us  [the longest x2 0.01 us: body(): gathered.append(lax.all_gather(slab, 'col', axis=0, tiled=True))]
    all_to_all x0 -> x1, blocking collectives: none -> 47.8 us  [body(): received = exchange(sent.reshape(devices, capacity, width))]
    pallas_call x0 -> x3, Pallas kernels: none -> 46.3 us  [the longest x2 33.7 us: send_rows(): pl.pallas_call(row_kernel, grid=(slots // tile,), in_specs=[pl.BlockSpec(...]
    dot_general x4 -> x6, matrix products: 46.3 us -> 10.2 us  [the longest x2 3.44 us: body(): jnp.dot(recv_hits, received.reshape(-1, width), preferred_element_type=F32)]
    reshape x2 -> x1, local copies, waits for them, and re-layouts: 28.7 us -> 1.23 us  [send_rows(): block.reshape(-1, 1)]
    concatenate x7 -> x1, other arithmetic: 18 us -> 0.81 us  [body(): slab = jnp.concatenate(slabs, axis=1)]
    another operation x3 -> x1, other arithmetic: 9.25 us -> 0.02 us
  transfers between devices with their start and end apart: 4 -> 7, of which waited for: 1 -> 1; matrix products, arithmetic and copies ran while one was open for 15% -> 12% of each run, Pallas kernels for 38% -> 51%
where the time goes in v1:
time: 332 us; the launch traced here: 331 us
  Pallas kernels  181 us (55%)
  blocking collectives  62.4 us (19%)
  matrix products  23.7 us (7%)
  starting transfers between devices  21.6 us (7%)
  between operations  15.3 us (5%)
  local copies, waits for them, and re-layouts  14 us (4%)
  waiting for transfers between devices  6.91 us (2%)
  other arithmetic  6.71 us (2%)
    pallas_call x1, Pallas kernels, inverse_factor(): pl.pallas_call(functools.partial(factor_kernel, block), in_specs=[pl.Bloc...  54.8 us
    pallas_call x2, Pallas kernels, group_table(): pl.pallas_call(functools.partial(group_kernel, block_count, tile), grid_s...  54 us
    all_to_all x1, blocking collectives, body(): received = exchange(sent.reshape(devices, capacity, width))  47.8 us
    pallas_call x2, Pallas kernels, send_rows(): pl.pallas_call(row_kernel, grid=(slots // tile,), in_specs=[pl.BlockSpec(...  33.7 us
    pallas_call x1, Pallas kernels, own_table(): pl.pallas_call(functools.partial(own_kernel, block_count), grid_spec=pltp...  25.6 us
    all_gather x1, blocking collectives, body(): column_part = lax.all_gather(row_part, 'col', axis=0, tiled=True)  14.7 us
    pallas_call x1, Pallas kernels, update(): pl.pallas_call(functools.partial(update_kernel, len(row_parts)), grid=(ro...  12.6 us
    dot_general x1, matrix products, body(): lax.dot_general(own_rows, panel_blocks, (((1,), (1,)), ((), ())), preferr...  9.1 us
  transfers between devices with their start and end apart: 7, of which 1 were waited for; matrix products, arithmetic and copies ran while one was open for 12% of the time, Pallas kernels for 51%

profile of v1, /device:TPU:0, one launch (start us, length us, event | category | flops | bytes accessed | tf_op | source)
XLA Modules:
  0.0 331.4 jit_solution(11809413058204412684)
XLA Ops:
  9.8 2.2 fusion.8
  12.8 7.3 %all-to-all-start = ((s32[32,1,56]{2,1,0:T(1,128)}), s32[32,1,56]{2,1,0:T(1,128)S(1)}, u32[]{:S(2)}, u32[]{:S(2)}) async-start(s32[32,1,56]{2,1,0:T(1,128)} %bitcast.1), calls=%async_computation | async-start | bytes 32768 | tf_op jit(solution)/shard_map/all_to_all | solution.py:446
  20.9 1.6 constant_dynamic-slice_fusion.panel_ref
  22.4 25.6 %own_table.1 = bf16[1024,4096]{1,0:T(8,128)(2,1)} custom-call(s32[16]{0:T(128)} %dynamic_slice.11.pos_ref, f32[512,512]{1,0:T(8,128)} %x_ref.3, f32[512,512]{1,0:T(8,128)} %y_ref.5, bf16[16,4096]{1,0:T(8,128)(2,1)} %constant_dynamic-slice_fusion.panel_ref), custom_call_target="tpu_custom_call" | custom-call | flops 15000000512 | bytes 10000000 | tf_op jit(solution)/shard_map/own_table/pallas_call | solution.py:220
  48.0 9.1 %select_reduce_fusion = f32[16,512]{1,0:T(8,128)S(1)} fusion(pred[64,512]{1,0:T(8,128)(4,1)S(1)} %iota_compare_fusion.19, bf16[1024,4096]{1,0:T(8,128)(2,1)} %own_table.1, bf16[512,4096]{1,0:T(8,128)(2,1)} %param.12), kind=kOutput, calls=%fused_computation.20 | convolution fusion | flops 4296007680 | bytes 12648448 | tf_op jit(solution)/shard_map/dot_general | solution.py:451
  57.1 14.7 %all_gather.12 = f32[64,512]{1,0:T(8,128)} all-gather(f32[16,512]{1,0:T(8,128)S(1)} %select_reduce_fusion), channel_id=1, replica_groups=mesh['row'=8,'col'=4] {'col'}, dimensions={0}, use_global_device_ids=true | all-gather | bytes 163840 | tf_op jit(solution)/shard_map/all_gather | solution.py:460
  73.0 4.8 %fusion.60 = (bf16[256,4096]{1,0:T(8,128)(2,1)}, bf16[256,4096]{1,0:T(8,128)(2,1)}) fusion(bf16[512,4096]{1,0:T(8,128)(2,1)} %param.12), kind=kLoop, calls=%fused_computation.102 | loop fusion | bytes 8388608 | tf_op jit(solution)/shard_map/slice | solution.py:472
  79.8 27.0 %group_table.2.table_ref = bf16[2,256,4096]{2,1,0:T(8,128)(2,1)} custom-call(s32[256]{0:T(256)} %get-tuple-element.19.pos_ref, s32[2]{0:T(128)} %dynamic-slice_reduce_fusion.own_ref, f32[512,512]{1,0:T(8,128)} %x_ref.3, f32[512,512]{1,0:T(8,128)} %y_ref.5, bf16[256,4096]{1,0:T(8,128)(2,1)} %get-tuple-element.9.panel_ref), custom_call_target="tpu_custom_call" | custom-call | flops 24999999488 | bytes 10000000 | tf_op jit(solution)/shard_map/group_table/pallas_call | solution.py:131
  106.8 16.9 %send_rows.2 = bf16[1792,256]{1,0:T(8,128)(2,1)} custom-call(bf16[1792,4096]{1,0:T(8,128)(2,1)} %cons_ref.3, bf16[2,256,4096]{2,1,0:T(8,128)(2,1)} %group_table.2.table_ref, s32[1792,1]{1,0:T(8,128)} %reshape.103.block_ref, s32[1,1792]{1,0:T(1,128)} %broadcast_in_dim.55.place_ref), custom_call_target="tpu_custom_call" | custom-call | flops 20000000000 | bytes 20000000 | tf_op jit(solution)/shard_map/send_rows/pallas_call | solution.py:272
  123.7 5.8 %all-to-all-start.1 = ((bf16[32,56,256]{2,1,0:T(8,128)(2,1)}), bf16[32,56,256]{2,1,0:T(8,128)(2,1)S(1)}, u32[]{:S(2)}, u32[]{:S(2)}) async-start(bf16[32,56,256]{2,1,0:T(8,128)(2,1)} %bitcast.30), calls=%async_computation.1 | async-start | bytes 1835008 | tf_op jit(solution)/shard_map/all_to_all | solution.py:475
  129.5 27.0 %group_table.3.table_ref = bf16[2,256,4096]{2,1,0:T(8,128)(2,1)} custom-call(s32[256]{0:T(256)} %get-tuple-element.20.pos_ref, s32[2]{0:T(128)} %dynamic-slice_reduce_fusion.own_ref, f32[512,512]{1,0:T(8,128)} %x_ref.3, f32[512,512]{1,0:T(8,128)} %y_ref.5, bf16[256,4096]{1,0:T(8,128)(2,1)} %get-tuple-element.8.panel_ref), custom_call_target="tpu_custom_call" | custom-call | flops 24999999488 | bytes 10000000 | tf_op jit(solution)/shard_map/group_table/pallas_call | solution.py:131
  157.8 2.1 fusion.17
  160.0 16.9 %send_rows.3 = bf16[1792,256]{1,0:T(8,128)(2,1)} custom-call(bf16[1792,4096]{1,0:T(8,128)(2,1)} %cons_ref.3, bf16[2,256,4096]{2,1,0:T(8,128)(2,1)} %group_table.3.table_ref, s32[1792,1]{1,0:T(8,128)} %reshape.103.block_ref, s32[1,1792]{1,0:T(1,128)} %broadcast_in_dim.55.place_ref), custom_call_target="tpu_custom_call" | custom-call | flops 20000000000 | bytes 20000000 | tf_op jit(solution)/shard_map/send_rows/pallas_call | solution.py:272
  176.9 47.8 %all_to_all.26 = bf16[32,56,256]{2,1,0:T(8,128)(2,1)S(1)} all-to-all(bf16[32,56,256]{2,1,0:T(8,128)(2,1)} %bitcast.32), channel_id=1, replica_groups=mesh['row'=8,'col'=4] {'row','col'}, dimensions={0} | all-to-all | bytes 1835008 | tf_op jit(solution)/shard_map/all_to_all | solution.py:475
  224.6 1.3 fusion.18
  226.9 4.9 %all-to-all-start.3 = ((bf16[4,64,512]{2,1,0:T(8,128)(2,1)}), bf16[4,64,512]{2,1,0:T(8,128)(2,1)S(1)}, u32[]{:S(2)}, u32[]{:S(2)}) async-start(bf16[4,64,512]{2,1,0:T(8,128)(2,1)} %bitcast.8), calls=%async_computation.3 | async-start | bytes 524288 | tf_op jit(solution)/shard_map/all_to_all | solution.py:486
  231.8 1.6 copy.25
  233.4 2.0 select_reduce_fusion.1
  237.2 54.8 %inverse_factor.1 = f32[512,512]{1,0:T(8,128)} custom-call(f32[512,512]{1,0:T(8,128)} %select_add_fusion.s_ref), custom_call_target="tpu_custom_call" | custom-call | flops 60000002048 | bytes 2000000 | tf_op jit(solution)/shard_map/inverse_factor/pallas_call | solution.py:384
  292.1 4.4 %reduce-precision_convert_fusion.1 = (bf16[512,512]{0,1:T(8,128)(2,1)S(1)}, bf16[512,512]{0,1:T(8,128)(2,1)}) fusion(f32[512,512]{1,0:T(8,128)} %inverse_factor.1), kind=kOutput, calls=%fused_computation.24 | convolution fusion | flops 1611923456 | bytes 2097152 | tf_op jit(solution)/shard_map/dot_general | solution.py:311
  297.3 3.5 %all-to-all-start.4 = ((bf16[8,64,512]{2,1,0:T(8,128)(2,1)}), bf16[8,64,512]{2,1,0:T(8,128)(2,1)S(1)}, u32[]{:S(2)}, u32[]{:S(2)}) async-start(bf16[8,64,512]{2,1,0:T(8,128)(2,1)} %broadcast_in_dim.59), calls=%async_computation.4 | async-start | bytes 1048576 | tf_op jit(solution)/shard_map/all_to_all | solution.py:487
  301.0 2.6 fusion.9
  303.6 6.8 %all-to-all-done.4 = bf16[8,64,512]{2,1,0:T(8,128)(2,1)S(1)} async-done(((bf16[8,64,512]{2,1,0:T(8,128)(2,1)}), bf16[8,64,512]{2,1,0:T(8,128)(2,1)S(1)}, u32[]{:S(2)}, u32[]{:S(2)}) %all-to-all-start.4) | async-done | bytes 524320 | tf_op jit(solution)/shard_map/all_to_all | solution.py:487
  312.3 12.6 %update.1 = f32[4096,512]{1,0:T(8,128)} custom-call(bf16[4096,256]{1,0:T(8,128)(2,1)} %all-gather.6.cloned.1.call-done.refs_0_, bf16[4096,256]{1,0:T(8,128)(2,1)} %all-gather.8.cloned.1.call-done.refs_1_, bf16[1024,512]{1,0:T(8,128)(2,1)} %maximum_bitcast_fusion.refs_2_, f32[4096,512]{1,0:T(8,128)} %refs_3_.1), custom_call_target="tpu_custom_call" | custom-call | flops 8000000000 | bytes 20000000 | tf_op jit(solution)/shard_map/update/pallas_call | solution.py:298
  (59 shorter events, 12.9 us)
Async XLA Ops:
  7.2 71.9 %copy-start = (s32[32,2]{0,1:T(2,128)S(1)}, s32[32,2]{0,1:T(2,128)}, u32[]{:S(2)}) copy-start(s32[32,2]{0,1:T(2,128)} %param.14) | copy-start | bytes 772
  7.2 2.6 copy-start.8
  9.8 10.4 %copy-start.10 = (s32[512]{0:T(512)S(1)}, s32[512]{0:T(512)}, u32[]{:S(2)}) copy-start(s32[512]{0:T(512)} %param.13) | copy-start | bytes 6148
  12.8 110.9 %all-to-all-start = ((s32[32,1,56]{2,1,0:T(1,128)}), s32[32,1,56]{2,1,0:T(1,128)S(1)}, u32[]{:S(2)}, u32[]{:S(2)}) async-start(s32[32,1,56]{2,1,0:T(1,128)} %bitcast.1), calls=%async_computation | async-start | bytes 32768 | tf_op jit(solution)/shard_map/all_to_all | solution.py:446
  20.1 211.6 %all-gather.4.cloned.1.call-start = ((), (), s32[]{:S(2)}) async-start(), calls=%async_computation.5 | async-start | bytes 1179648 | tf_op jit(solution)/shard_map/all_gather | solution.py:461
  73.0 4.8 %copy-start.9 = (s32[1792]{0:T(1024)S(1)}, s32[1792]{0:T(1024)}, u32[]{:S(2)}) copy-start(s32[1792]{0:T(1024)} %param.16) | copy-start | bytes 21508
  123.7 34.1 %all-to-all-start.1 = ((bf16[32,56,256]{2,1,0:T(8,128)(2,1)}), bf16[32,56,256]{2,1,0:T(8,128)(2,1)S(1)}, u32[]{:S(2)}, u32[]{:S(2)}) async-start(bf16[32,56,256]{2,1,0:T(8,128)(2,1)} %bitcast.30), calls=%async_computation.1 | async-start | bytes 1835008 | tf_op jit(solution)/shard_map/all_to_all | solution.py:475
  129.5 182.8 %all-gather.6.cloned.1.call-start = ((), (), s32[]{:S(2)}) async-start(), calls=%async_computation.6 | async-start | bytes 2621440 | tf_op jit(solution)/shard_map/all_gather | solution.py:481
  160.0 152.3 %all-gather.8.cloned.1.call-start = ((), (), s32[]{:S(2)}) async-start(), calls=%async_computation.7 | async-start | bytes 2621440 | tf_op jit(solution)/shard_map/all_gather | solution.py:481
  224.6 1.3 copy-start.4
  225.9 0.9 copy-start.5
  226.9 69.6 %all-to-all-start.3 = ((bf16[4,64,512]{2,1,0:T(8,128)(2,1)}), bf16[4,64,512]{2,1,0:T(8,128)(2,1)S(1)}, u32[]{:S(2)}, u32[]{:S(2)}) async-start(bf16[4,64,512]{2,1,0:T(8,128)(2,1)} %bitcast.8), calls=%async_computation.3 | async-start | bytes 524288 | tf_op jit(solution)/shard_map/all_to_all | solution.py:486
  231.7 4.3 %copy-start.2 = (f32[512,512]{1,0:T(8,128)S(1)}, f32[512,512]{1,0:T(8,128)}, u32[]{:S(2)}) copy-start(f32[512,512]{1,0:T(8,128)} %all-gather.4.cloned.1.call-done) | copy-start | bytes 3145732
  292.1 8.7 %copy-start.3 = (f32[512,512]{1,0:T(8,128)S(1)}, f32[512,512]{1,0:T(8,128)}, u32[]{:S(2)}) copy-start(f32[512,512]{1,0:T(8,128)} %inverse_factor.1) | copy-start | bytes 3145732
  292.1 8.9 %copy-start.6 = (bf16[1024,256]{1,0:T(8,128)(2,1)S(1)}, bf16[1024,256]{1,0:T(8,128)(2,1)}, u32[]{:S(2)}) copy-start(bf16[1024,256]{1,0:T(8,128)(2,1)} %copy-done.5) | copy-start | bytes 1572868
  297.3 13.1 %all-to-all-start.4 = ((bf16[8,64,512]{2,1,0:T(8,128)(2,1)}), bf16[8,64,512]{2,1,0:T(8,128)(2,1)S(1)}, u32[]{:S(2)}, u32[]{:S(2)}) async-start(bf16[8,64,512]{2,1,0:T(8,128)(2,1)} %broadcast_in_dim.59), calls=%async_computation.4 | async-start | bytes 1048576 | tf_op jit(solution)/shard_map/all_to_all | solution.py:487
  301.0 9.5 %copy-start.7 = (bf16[512,512]{0,1:T(8,128)(2,1)S(1)}, bf16[512,512]{0,1:T(8,128)(2,1)}, u32[]{:S(2)}) copy-start(bf16[512,512]{0,1:T(8,128)(2,1)} %get-tuple-element.13) | copy-start | bytes 1572868
  312.3 12.6 %copy-start.1 = (s32[32,2]{0,1:T(2,128)S(1)}, s32[32,2]{0,1:T(2,128)}, u32[]{:S(2)}) copy-start(s32[32,2]{0,1:T(2,128)} %param.14) | copy-start | bytes 772
Sparse Core Ops, SparseCore 0:
  72.0 24.5 all-gather.3
  160.1 66.5 all-gather.5
  228.3 48.0 all-gather.7

commit v2 on v1

--- a/solution.py
+++ b/solution.py
@@ -8,6 +8,7 @@
 from jax.experimental.pallas import tpu as pltpu
 from jax.sharding import PartitionSpec as P
 
+
 BF16 = jnp.bfloat16
 F32 = jnp.float32
 
@@ -17,8 +18,10 @@
     low = (value - high.astype(F32)).astype(BF16)
     return high, low
 
+
 def lane_half(rows, width):
     return lax.broadcasted_iota(jnp.int32, (rows, width), 1) < width // 2
+
 
 def unpack_pairs(panel_ref, pairs, count, block_size):
     lanes = 2 * block_size
@@ -30,11 +33,13 @@
         pairs[pl.ds(2 * c, count, stride=pitch), :] = jnp.where(keep, both, turned)
         pairs[pl.ds(2 * c + 1, count, stride=pitch), :] = jnp.where(keep, turned, both)
 
+
 def column_block(ref, block, slot, block_size):
     lanes = 2 * block_size
     start = pl.multiple_of(block // 2 * lanes, lanes)
     wide = ref[:, pl.ds(start, lanes)]
     return jnp.where(block % 2 == slot, wide, pltpu.roll(wide, block_size, 1))
+
 
 def group_kernel(block_count, tile, pos_ref, own_ref, x_ref, y_ref, panel_ref, out_ref, left, right, pairs, scr, mid):
     step = pl.program_id(0)
@@ -115,6 +120,7 @@
         columns = slice(r * block_size, (r + 2) * block_size)
         out_ref[0, :, columns] = jnp.where(keep_t, even, pltpu.roll(odd, block_size, 1)).astype(BF16)
         out_ref[1, :, columns] = jnp.where(keep_t, pltpu.roll(even, block_size, 1), odd).astype(BF16)
+
 
 def whole(shape):
     return pl.BlockSpec(shape, lambda *_: (0,) * len(shape))
@@ -314,11 +320,17 @@
     )
 
 
-def factor_kernel(block, s_ref, out_ref, a, work):
+def factor_kernel(block, begin, end, finish, *refs):
+    if finish:
+        s_ref, done_ref, out_ref, a, work = refs
+    else:
+        s_ref, a, out_ref, work = refs
     order = s_ref.shape[0]
     count = order // block
     groups = block // 8
     a[...] = s_ref[...]
+    if finish:
+        out_ref[...] = done_ref[...]
     row_id = lax.broadcasted_iota(jnp.int32, (8, 1), 0)
     eye = (
         lax.broadcasted_iota(jnp.int32, (block, block), 0)
@@ -365,7 +377,9 @@
 
         return carry
 
-    lax.fori_loop(0, count, body, 0)
+    lax.fori_loop(begin, end, body, 0)
+    if not finish:
+        return
     for i in range(count):
         for b in range(i + 1, count):
             out_ref[i * block : (i + 1) * block, b * block : (b + 1) * block] = jnp.zeros(
@@ -378,20 +392,33 @@
         out_ref[i * block : (i + 1) * block, : i * block] = -hdot(own, total, (1, 0))
 
 
-def inverse_factor(matrix):
+def factor_start(matrix):
+    order = matrix.shape[0]
+    block = 128
+    shape = jax.ShapeDtypeStruct((order, order), F32)
+    return pl.pallas_call(
+        functools.partial(factor_kernel, block, 0, order // block // 2, False),
+        in_specs=[pl.BlockSpec(memory_space=pltpu.VMEM)],
+        out_specs=[pl.BlockSpec(memory_space=pltpu.VMEM)] * 2,
+        out_shape=[shape, shape],
+        scratch_shapes=[pltpu.VMEM((block, 2 * block), F32)],
+        cost_estimate=cost(30, 10**6),
+        name="factor_start",
+    )(matrix)
+
+
+def factor_end(matrix, done):
     order = matrix.shape[0]
     block = 128
     return pl.pallas_call(
-        functools.partial(factor_kernel, block),
-        in_specs=[pl.BlockSpec(memory_space=pltpu.VMEM)],
+        functools.partial(factor_kernel, block, order // block // 2, order // block, True),
+        in_specs=[pl.BlockSpec(memory_space=pltpu.VMEM)] * 2,
         out_specs=pl.BlockSpec(memory_space=pltpu.VMEM),
         out_shape=jax.ShapeDtypeStruct((order, order), F32),
         scratch_shapes=[pltpu.VMEM((order, order), F32), pltpu.VMEM((block, 2 * block), F32)],
-        cost_estimate=pl.CostEstimate(
-            flops=60 * 10**9, bytes_accessed=2 * 10**6, transcendentals=order
-        ),
-        name="inverse_factor",
-    )(matrix)
+        cost_estimate=cost(30, 10**6),
+        name="factor_end",
+    )(matrix, done)
 
 
 def body(
@@ -457,28 +484,44 @@
     row_part = jnp.sum(
         jnp.where(hit[None], products.reshape(per_device, position_count, panel_cols), 0.0), axis=1
     )
-    column_part = lax.all_gather(row_part, "col", axis=0, tiled=True)
-    panel_schur = lax.all_gather(column_part, "row", axis=0, tiled=True)
+    panel_schur = lax.all_gather(row_part, ("row", "col"), axis=0, tiled=True)
 
     own_group = lax.dynamic_index_in_dim(group_blocks, device_id, 0, keepdims=False)
     halves = 2
     width = panel_cols // halves
     token = row_part
     local_ids = jnp.arange(sub_rows, dtype=jnp.int32)
-    slabs, gathered = [], []
+    recv_hits = (local_ids[:, None] == recv_local.reshape(1, -1)).astype(BF16)
+
+    def settle(rows):
+        slab = jnp.dot(recv_hits, rows.reshape(-1, width), preferred_element_type=F32).astype(BF16)
+        return slab, lax.all_gather(slab, "col", axis=0, tiled=True)
+
+    received, settled = [], []
     for half in range(halves):
         cols = slice(half * width, (half + 1) * width)
         x_now, token = lax.optimization_barrier((x_mat, token))
         table = group_table(x_now, y_inv, panel_blocks[cols], panel_pos[cols], own_group, block_count)
+        if half:
+            settled.append(settle(received[-1]))
+            table, _ = lax.optimization_barrier((table, settled[-1][0]))
         sent = send_rows(cons_blocks, table, slot_block, slot_place, places)
         token = sent
-        received = exchange(sent.reshape(devices, capacity, width))
-        recv_hits = (local_ids[:, None] == recv_local.reshape(1, -1)).astype(BF16)
-        slab = jnp.dot(
-            recv_hits, received.reshape(-1, width), preferred_element_type=F32
-        ).astype(BF16)
-        slabs.append(slab)
-        gathered.append(lax.all_gather(slab, "col", axis=0, tiled=True))
+        received.append(exchange(sent.reshape(devices, capacity, width)))
+
+    panel_schur, token = lax.optimization_barrier((panel_schur, token))
+    symmetric = 0.5 * (panel_schur + panel_schur.T)
+    eye = (
+        lax.broadcasted_iota(jnp.int32, symmetric.shape, 0)
+        == lax.broadcasted_iota(jnp.int32, symmetric.shape, 1)
+    )
+    diag_shift = 0.01 * jnp.sum(jnp.where(eye, symmetric, 0.0)) / panel_cols
+    first = factor_start(symmetric + jnp.where(eye, diag_shift, 0.0))
+    last, first = lax.optimization_barrier((received[-1], first))
+    settled.append(settle(last))
+    slabs, gathered = zip(*settled)
+    first, token = lax.optimization_barrier((first, slabs[-1]))
+    inverse = factor_end(*first)
 
     block_rows = trailing.shape[1] // rows_size
     slab = jnp.concatenate(slabs, axis=1)
@@ -489,14 +532,6 @@
         "row", split_axis=0, concat_axis=0, tiled=True,
     ).reshape(rows_size * block_rows, panel_cols)
 
-    panel_schur, token = lax.optimization_barrier((panel_schur, token))
-    symmetric = 0.5 * (panel_schur + panel_schur.T)
-    eye = (
-        lax.broadcasted_iota(jnp.int32, symmetric.shape, 0)
-        == lax.broadcasted_iota(jnp.int32, symmetric.shape, 1)
-    )
-    diag_shift = 0.01 * jnp.sum(jnp.where(eye, symmetric, 0.0)) / panel_cols
-    inverse = inverse_factor(symmetric + jnp.where(eye, diag_shift, 0.0))
     inner = hdot(inverse, inverse, (0, 0))
 
     def doubled(matrix):

time: 332 us -> 291 us (0.88)
  blocking collectives: 62.4 us -> 0 us
  waiting for transfers between devices: 6.91 us -> 14.6 us
  starting transfers between devices: 21.6 us -> 28.3 us
    all_to_all x1 -> x0, blocking collectives: 47.8 us -> none  [body(): received = exchange(sent.reshape(devices, capacity, width))]
    all_gather x1 -> x0, blocking collectives: 14.7 us -> none  [body(): column_part = lax.all_gather(row_part, 'col', axis=0, tiled=True)]
    all_to_all x1 -> x2, waiting for transfers between devices: 0.01 us -> 7.69 us  [body(): received.append(exchange(sent.reshape(devices, capacity, width)))]
    all_to_all x1 -> x2, starting transfers between devices: 5.78 us -> 11.7 us  [body(): received.append(exchange(sent.reshape(devices, capacity, width)))]
    pallas_call x1 -> x2, Pallas kernels: 54.8 us -> 57.9 us  [the longest x1 29.2 us: factor_end(): pl.pallas_call(functools.partial(factor_kernel, block, order // block //...]
  transfers between devices with their start and end apart: 7 -> 8, of which waited for: 1 -> 2; matrix products, arithmetic and copies ran while one was open for 12% -> 14% of each run, Pallas kernels for 51% -> 60%
where the time goes in v2:
time: 291 us; the launch traced here: 287 us
  Pallas kernels  184 us (63%)
  starting transfers between devices  28.3 us (10%)
  matrix products  24.2 us (8%)
  between operations  15.6 us (5%)
  waiting for transfers between devices  14.6 us (5%)
  local copies, waits for them, and re-layouts  14.1 us (5%)
  other arithmetic  6.59 us (2%)
    pallas_call x2, Pallas kernels, group_table(): pl.pallas_call(functools.partial(group_kernel, block_count, tile), grid_s...  54 us
    pallas_call x2, Pallas kernels, send_rows(): pl.pallas_call(row_kernel, grid=(slots // tile,), in_specs=[pl.BlockSpec(...  33.7 us
    pallas_call x1, Pallas kernels, factor_end(): pl.pallas_call(functools.partial(factor_kernel, block, order // block //...  29.2 us
    pallas_call x1, Pallas kernels, factor_start(): pl.pallas_call(functools.partial(factor_kernel, block, 0, order // block...  28.7 us
    pallas_call x1, Pallas kernels, own_table(): pl.pallas_call(functools.partial(own_kernel, block_count), grid_spec=pltp...  25.6 us
    pallas_call x1, Pallas kernels, update(): pl.pallas_call(functools.partial(update_kernel, len(row_parts)), grid=(ro...  12.6 us
    all_to_all x2, starting transfers between devices, body(): received.append(exchange(sent.reshape(devices, capacity, width)))  11.7 us
    dot_general x1, matrix products, body(): lax.dot_general(own_rows, panel_blocks, (((1,), (1,)), ((), ())), preferr...  9.7 us
  transfers between devices with their start and end apart: 8, of which 2 were waited for; matrix products, arithmetic and copies ran while one was open for 14% of the time, Pallas kernels for 60%

profile of v2, /device:TPU:0, one launch (start us, length us, event | category | flops | bytes accessed | tf_op | source)
XLA Modules:
  0.0 287.2 jit_solution(16442776617825965404)
XLA Ops:
  9.8 2.2 fusion.8
  12.8 7.3 %all-to-all-start = ((s32[32,1,56]{2,1,0:T(1,128)}), s32[32,1,56]{2,1,0:T(1,128)S(1)}, u32[]{:S(2)}, u32[]{:S(2)}) async-start(s32[32,1,56]{2,1,0:T(1,128)} %bitcast.1), calls=%async_computation | async-start | bytes 32768 | tf_op jit(solution)/shard_map/all_to_all | solution.py:473
  21.4 1.6 constant_dynamic-slice_fusion.panel_ref
  22.9 25.6 %own_table.1 = bf16[1024,4096]{1,0:T(8,128)(2,1)} custom-call(s32[16]{0:T(128)} %dynamic_slice.11.pos_ref, f32[512,512]{1,0:T(8,128)} %x_ref.3, f32[512,512]{1,0:T(8,128)} %y_ref.5, bf16[16,4096]{1,0:T(8,128)(2,1)} %constant_dynamic-slice_fusion.panel_ref), custom_call_target="tpu_custom_call" | custom-call | flops 15000000512 | bytes 10000000 | tf_op jit(solution)/shard_map/own_table/pallas_call | solution.py:226
  48.5 9.7 %select_reduce_fusion = f32[16,512]{1,0:T(8,128)} fusion(pred[64,512]{1,0:T(8,128)(4,1)S(1)} %iota_compare_fusion.19, bf16[1024,4096]{1,0:T(8,128)(2,1)} %own_table.1, bf16[512,4096]{1,0:T(8,128)(2,1)} %param.12), kind=kOutput, calls=%fused_computation.20 | convolution fusion | flops 4296007680 | bytes 12648448 | tf_op jit(solution)/shard_map/dot_general | solution.py:478
  59.5 4.8 %fusion.60 = (bf16[256,4096]{1,0:T(8,128)(2,1)}, bf16[256,4096]{1,0:T(8,128)(2,1)}) fusion(bf16[512,4096]{1,0:T(8,128)(2,1)} %param.12), kind=kLoop, calls=%fused_computation.102 | loop fusion | bytes 8388608 | tf_op jit(solution)/shard_map/slice | solution.py:504
  66.2 27.0 %group_table.2.table_ref = bf16[2,256,4096]{2,1,0:T(8,128)(2,1)} custom-call(s32[256]{0:T(256)} %get-tuple-element.35.pos_ref, s32[2]{0:T(128)} %dynamic-slice_reduce_fusion.own_ref, f32[512,512]{1,0:T(8,128)} %x_ref.3, f32[512,512]{1,0:T(8,128)} %y_ref.5, bf16[256,4096]{1,0:T(8,128)(2,1)} %get-tuple-element.25.panel_ref), custom_call_target="tpu_custom_call" | custom-call | flops 24999999488 | bytes 10000000 | tf_op jit(solution)/shard_map/group_table/pallas_call | solution.py:137
  93.2 16.9 %send_rows.2 = bf16[1792,256]{1,0:T(8,128)(2,1)} custom-call(bf16[1792,4096]{1,0:T(8,128)(2,1)} %cons_ref.3, bf16[2,256,4096]{2,1,0:T(8,128)(2,1)} %group_table.2.table_ref, s32[1792,1]{1,0:T(8,128)} %reshape.102.block_ref, s32[1,1792]{1,0:T(1,128)} %broadcast_in_dim.54.place_ref), custom_call_target="tpu_custom_call" | custom-call | flops 20000000000 | bytes 20000000 | tf_op jit(solution)/shard_map/send_rows/pallas_call | solution.py:278
  110.1 5.8 %all-to-all-start.1 = ((bf16[32,56,256]{2,1,0:T(8,128)(2,1)}), bf16[32,56,256]{2,1,0:T(8,128)(2,1)S(1)}, u32[]{:S(2)}, u32[]{:S(2)}) async-start(bf16[32,56,256]{2,1,0:T(8,128)(2,1)} %bitcast.32), calls=%async_computation.1 | async-start | bytes 1835008 | tf_op jit(solution)/shard_map/all_to_all | solution.py:510
  116.1 27.0 %group_table.3.table_ref = bf16[2,256,4096]{2,1,0:T(8,128)(2,1)} custom-call(s32[256]{0:T(256)} %get-tuple-element.36.pos_ref, s32[2]{0:T(128)} %dynamic-slice_reduce_fusion.own_ref, f32[512,512]{1,0:T(8,128)} %x_ref.3, f32[512,512]{1,0:T(8,128)} %y_ref.5, bf16[256,4096]{1,0:T(8,128)(2,1)} %get-tuple-element.24.panel_ref), custom_call_target="tpu_custom_call" | custom-call | flops 24999999488 | bytes 10000000 | tf_op jit(solution)/shard_map/group_table/pallas_call | solution.py:137
  144.4 2.1 fusion.17
  146.6 16.9 %send_rows.3 = bf16[1792,256]{1,0:T(8,128)(2,1)} custom-call(bf16[1792,4096]{1,0:T(8,128)(2,1)} %cons_ref.3, bf16[2,256,4096]{2,1,0:T(8,128)(2,1)} %group_table.3.table_ref, s32[1792,1]{1,0:T(8,128)} %reshape.102.block_ref, s32[1,1792]{1,0:T(1,128)} %broadcast_in_dim.54.place_ref), custom_call_target="tpu_custom_call" | custom-call | flops 20000000000 | bytes 20000000 | tf_op jit(solution)/shard_map/send_rows/pallas_call | solution.py:278
  163.5 5.8 %all-to-all-start.2 = ((bf16[32,56,256]{2,1,0:T(8,128)(2,1)}), bf16[32,56,256]{2,1,0:T(8,128)(2,1)S(1)}, u32[]{:S(2)}, u32[]{:S(2)}) async-start(bf16[32,56,256]{2,1,0:T(8,128)(2,1)} %bitcast.31), calls=%async_computation.2 | async-start | bytes 1835008 | tf_op jit(solution)/shard_map/all_to_all | solution.py:510
  169.4 1.6 copy.24
  171.0 1.9 select_reduce_fusion.1
  174.8 28.7 %factor_start.1 = (f32[512,512]{1,0:T(8,128)}, f32[512,512]{1,0:T(8,128)}) custom-call(f32[512,512]{1,0:T(8,128)} %select_add_fusion.refs_0_), custom_call_target="tpu_custom_call" | custom-call | flops 30000001024 | bytes 1000000 | tf_op jit(solution)/shard_map/factor_start/pallas_call | solution.py:399
  203.5 7.7 %all-to-all-done.2 = bf16[32,56,256]{2,1,0:T(8,128)(2,1)S(1)} async-done(((bf16[32,56,256]{2,1,0:T(8,128)(2,1)}), bf16[32,56,256]{2,1,0:T(8,128)(2,1)S(1)}, u32[]{:S(2)}, u32[]{:S(2)}) %all-to-all-start.2) | async-done | bytes 917536 | tf_op jit(solution)/shard_map/all_to_all | solution.py:510
  213.5 5.1 %all-to-all-start.3 = ((bf16[4,64,512]{2,1,0:T(8,128)(2,1)}), bf16[4,64,512]{2,1,0:T(8,128)(2,1)S(1)}, u32[]{:S(2)}, u32[]{:S(2)}) async-start(bf16[4,64,512]{2,1,0:T(8,128)(2,1)} %bitcast.8), calls=%async_computation.3 | async-start | bytes 524288 | tf_op jit(solution)/shard_map/all_to_all | solution.py:529
  218.6 29.2 %factor_end.1 = f32[512,512]{1,0:T(8,128)} custom-call(f32[512,512]{1,0:T(8,128)} %get-tuple-element.22.refs_0_, f32[512,512]{1,0:T(8,128)} %get-tuple-element.23.refs_1_), custom_call_target="tpu_custom_call" | custom-call | flops 30000001024 | bytes 1000000 | tf_op jit(solution)/shard_map/factor_end/pallas_call | solution.py:413
  247.7 4.3 %reduce-precision_convert_fusion.1 = (bf16[512,512]{0,1:T(8,128)(2,1)S(1)}, bf16[512,512]{0,1:T(8,128)(2,1)}) fusion(f32[512,512]{1,0:T(8,128)} %factor_end.1), kind=kOutput, calls=%fused_computation.24 | convolution fusion | flops 1611923456 | bytes 2097152 | tf_op jit(solution)/shard_map/dot_general | solution.py:317
  252.9 3.5 %all-to-all-start.4 = ((bf16[8,64,512]{2,1,0:T(8,128)(2,1)}), bf16[8,64,512]{2,1,0:T(8,128)(2,1)S(1)}, u32[]{:S(2)}, u32[]{:S(2)}) async-start(bf16[8,64,512]{2,1,0:T(8,128)(2,1)} %broadcast_in_dim.58), calls=%async_computation.4 | async-start | bytes 1048576 | tf_op jit(solution)/shard_map/all_to_all | solution.py:530
  256.6 2.6 fusion.9
  259.2 6.8 %all-to-all-done.4 = bf16[8,64,512]{2,1,0:T(8,128)(2,1)S(1)} async-done(((bf16[8,64,512]{2,1,0:T(8,128)(2,1)}), bf16[8,64,512]{2,1,0:T(8,128)(2,1)S(1)}, u32[]{:S(2)}, u32[]{:S(2)}) %all-to-all-start.4) | async-done | bytes 524320 | tf_op jit(solution)/shard_map/all_to_all | solution.py:530
  267.9 12.6 %update.1 = f32[4096,512]{1,0:T(8,128)} custom-call(bf16[4096,256]{1,0:T(8,128)(2,1)} %all-gather.6.cloned.1.call-done.refs_0_, bf16[4096,256]{1,0:T(8,128)(2,1)} %all-gather.8.cloned.1.call-done.refs_1_, bf16[1024,512]{1,0:T(8,128)(2,1)} %maximum_bitcast_fusion.refs_2_, f32[4096,512]{1,0:T(8,128)} %refs_3_.1), custom_call_target="tpu_custom_call" | custom-call | flops 8000000000 | bytes 20000000 | tf_op jit(solution)/shard_map/update/pallas_call | solution.py:304
  (60 shorter events, 14.9 us)
Async XLA Ops:
  7.2 58.3 %copy-start = (s32[32,2]{0,1:T(2,128)S(1)}, s32[32,2]{0,1:T(2,128)}, u32[]{:S(2)}) copy-start(s32[32,2]{0,1:T(2,128)} %param.14) | copy-start | bytes 772
  7.2 2.6 copy-start.8
  9.8 10.9 %copy-start.10 = (s32[512]{0:T(512)S(1)}, s32[512]{0:T(512)}, u32[]{:S(2)}) copy-start(s32[512]{0:T(512)} %param.13) | copy-start | bytes 6148
  12.8 97.3 %all-to-all-start = ((s32[32,1,56]{2,1,0:T(1,128)}), s32[32,1,56]{2,1,0:T(1,128)S(1)}, u32[]{:S(2)}, u32[]{:S(2)}) async-start(s32[32,1,56]{2,1,0:T(1,128)} %bitcast.1), calls=%async_computation | async-start | bytes 32768 | tf_op jit(solution)/shard_map/all_to_all | solution.py:473
  20.1 149.2 %all-gather.4.cloned.1.call-start = ((), (), s32[]{:S(2)}) async-start(), calls=%async_computation.5 | async-start | bytes 1081344 | tf_op jit(solution)/shard_map/all_gather | solution.py:487
  59.5 4.8 %copy-start.9 = (s32[1792]{0:T(1024)S(1)}, s32[1792]{0:T(1024)}, u32[]{:S(2)}) copy-start(s32[1792]{0:T(1024)} %param.16) | copy-start | bytes 21508
  110.1 34.3 %all-to-all-start.1 = ((bf16[32,56,256]{2,1,0:T(8,128)(2,1)}), bf16[32,56,256]{2,1,0:T(8,128)(2,1)S(1)}, u32[]{:S(2)}, u32[]{:S(2)}) async-start(bf16[32,56,256]{2,1,0:T(8,128)(2,1)} %bitcast.32), calls=%async_computation.1 | async-start | bytes 1835008 | tf_op jit(solution)/shard_map/all_to_all | solution.py:510
  115.9 151.9 %all-gather.6.cloned.1.call-start = ((), (), s32[]{:S(2)}) async-start(), calls=%async_computation.6 | async-start | bytes 2621440 | tf_op jit(solution)/shard_map/all_gather | solution.py:498
  163.5 47.8 %all-to-all-start.2 = ((bf16[32,56,256]{2,1,0:T(8,128)(2,1)}), bf16[32,56,256]{2,1,0:T(8,128)(2,1)S(1)}, u32[]{:S(2)}, u32[]{:S(2)}) async-start(bf16[32,56,256]{2,1,0:T(8,128)(2,1)} %bitcast.31), calls=%async_computation.2 | async-start | bytes 1835008 | tf_op jit(solution)/shard_map/all_to_all | solution.py:510
  169.3 98.6 %all-gather.8.cloned.1.call-start = ((), (), s32[]{:S(2)}) async-start(), calls=%async_computation.7 | async-start | bytes 2621440 | tf_op jit(solution)/shard_map/all_gather | solution.py:498
  169.4 4.2 %copy-start.2 = (f32[512,512]{1,0:T(8,128)S(1)}, f32[512,512]{1,0:T(8,128)}, u32[]{:S(2)}) copy-start(f32[512,512]{1,0:T(8,128)} %all-gather.4.cloned.1.call-done) | copy-start | bytes 3145732
  211.2 1.3 copy-start.4
  212.5 0.9 copy-start.5
  213.5 38.6 %all-to-all-start.3 = ((bf16[4,64,512]{2,1,0:T(8,128)(2,1)}), bf16[4,64,512]{2,1,0:T(8,128)(2,1)S(1)}, u32[]{:S(2)}, u32[]{:S(2)}) async-start(bf16[4,64,512]{2,1,0:T(8,128)(2,1)} %bitcast.8), calls=%async_computation.3 | async-start | bytes 524288 | tf_op jit(solution)/shard_map/all_to_all | solution.py:529
  247.7 8.7 %copy-start.3 = (f32[512,512]{1,0:T(8,128)S(1)}, f32[512,512]{1,0:T(8,128)}, u32[]{:S(2)}) copy-start(f32[512,512]{1,0:T(8,128)} %factor_end.1) | copy-start | bytes 3145732
  247.7 8.9 %copy-start.6 = (bf16[1024,256]{1,0:T(8,128)(2,1)S(1)}, bf16[1024,256]{1,0:T(8,128)(2,1)}, u32[]{:S(2)}) copy-start(bf16[1024,256]{1,0:T(8,128)(2,1)} %copy-done.5) | copy-start | bytes 1572868
  252.9 13.1 %all-to-all-start.4 = ((bf16[8,64,512]{2,1,0:T(8,128)(2,1)}), bf16[8,64,512]{2,1,0:T(8,128)(2,1)S(1)}, u32[]{:S(2)}, u32[]{:S(2)}) async-start(bf16[8,64,512]{2,1,0:T(8,128)(2,1)} %broadcast_in_dim.58), calls=%async_computation.4 | async-start | bytes 1048576 | tf_op jit(solution)/shard_map/all_to_all | solution.py:530
  256.6 9.5 %copy-start.7 = (bf16[512,512]{0,1:T(8,128)(2,1)S(1)}, bf16[512,512]{0,1:T(8,128)(2,1)}, u32[]{:S(2)}) copy-start(bf16[512,512]{0,1:T(8,128)(2,1)} %get-tuple-element.29) | copy-start | bytes 1572868
  267.9 12.6 %copy-start.1 = (s32[32,2]{0,1:T(2,128)S(1)}, s32[32,2]{0,1:T(2,128)}, u32[]{:S(2)}) copy-start(s32[32,2]{0,1:T(2,128)} %param.14) | copy-start | bytes 772
Sparse Core Ops, SparseCore 0:
  58.4 55.0 all-gather.3
  146.7 66.5 all-gather.5
  214.9 47.1 all-gather.7
